TPU v7x, 512 devices: a whole 4x4x16 slice. The times are simulated.
512 devices in a mesh: ctx: 64 (over z, y_hi, core), tp: 8 (over x, y_lo).
Axes of the slice: x: 4, y: 4 (y_hi: 2, y_lo: 2; y = y_hi * 2 + y_lo), z: 16, core: 2. Of those that a mesh axis runs over, the one named last changes fastest.
Arguments:
- queries: bfloat16 [8192, 8192], P('ctx', 'tp'), may hold values from -8 to 8
- keys: bfloat16 [8192, 1024], P('ctx', 'tp'), may hold values from -4 to 4
- values: bfloat16 [8192, 1024], P('ctx', 'tp'), may hold values from -4 to 4
- attn_out: bfloat16 [8192, 8192], P('ctx', 'tp'), may hold values from -4 to 4, as said below
- out_grad: bfloat16 [8192, 8192], P(('ctx', 'tp')), may hold values from -24 to 24
- logsumexp: float32 [64, 8192], P('tp', 'ctx'), may hold values from -50 to 50, as said below
- position_ids: int32 [3, 8192], P(None, 'ctx'), may hold values from 0 to 8191, as said below
- block_map: int32 [128], replicated, may hold values from 0 to 127, as said below
- span_blocks: int32 [16, 2], replicated, may hold values from 0 to 127, as said below
Outputs:
- grad_q: bfloat16 [8192, 8192], P('ctx', 'tp')
- key_gradient: bfloat16 [8192, 1024], P('ctx', 'tp')
- value_gradient: bfloat16 [8192, 1024], P('ctx', 'tp')
Inputs may be any that keep to these rules, and one draw needn't show every extreme that they name: `block_map`: a permutation of the sequence blocks. `span_blocks`: spans ascend in sequence order and do not intersect; each row is a start block and an end block past the span's last; the first span starts at block 0 and the last ends at block 127. `position_ids`: given inputs, not renumbered after spans: text rows carry their sequence position in all three ids; a row of a visual span carries the span's first position plus its frame, grid row and grid column. `attn_out`: the output of the forward pass for these queries, keys and values. `logsumexp`: the log of each row's softmax total over its allowed keys, from the forward pass.
All inputs are finite; a program needn't handle non-finite values.
Results may differ from a plain program's by a relative error of at most 0.011.
Values may be sent and summed in bfloat16 or wider, within the bound.
A program may use at most 64 MiB of HBM per device.

v0:
```python
import math

import jax
import jax.numpy as jnp
from jax import lax
from jax.sharding import PartitionSpec as P

HEAD_SIZE = 128
BLOCKS_DEV = 2


THETA = 1000000.0


def passed_along(block, axis, distance):
    devices = range(lax.axis_size(axis))
    route = [((i - distance) % len(devices), i) for i in devices]
    return lax.ppermute(block, axis, route)


def rope_tables(position_ids, width):
    half_width = width // 2
    pair_index = jnp.arange(half_width, dtype=jnp.int32)
    first_cut = width // 8
    second_cut = first_cut + 3 * width // 16
    inverse = jnp.exp(pair_index.astype(jnp.float32) * jnp.float32(-2.0 * math.log(THETA) / width))
    picked = jnp.where(
        pair_index[None, :] < first_cut,
        position_ids[0][:, None],
        jnp.where(
            pair_index[None, :] < second_cut, position_ids[1][:, None], position_ids[2][:, None]
        ),
    )
    angles = picked.astype(jnp.float32) * inverse[None, :]
    cosine_table = jnp.concatenate([jnp.cos(angles), jnp.cos(angles)], axis=-1)
    sine_lookup = jnp.concatenate([jnp.sin(angles), jnp.sin(angles)], axis=-1)
    return (cosine_table, sine_lookup)


def apply_rotation(field, cosine_table, sine_lookup):
    half_width = field.shape[-1] // 2
    turned = jnp.concatenate([-field[..., half_width:], field[..., :half_width]], axis=-1)
    return field * cosine_table[:, None, :] + turned * sine_lookup[:, None, :]


def reverse_rotation(field, cosine_table, sine_lookup):
    half_width = field.shape[-1] // 2
    scaled = field * sine_lookup[:, None, :]
    turned = jnp.concatenate([scaled[..., half_width:], -scaled[..., :half_width]], axis=-1)
    return field * cosine_table[:, None, :] + turned


def heads_first(field, kv_heads, query_group_width):
    row_count = field.shape[0]
    return field.reshape(row_count, kv_heads, query_group_width, HEAD_SIZE).transpose(1, 2, 0, 3)


def shards(
    queries, keys, values, attn_out, out_grad, logsumexp, position_ids, block_map, span_blocks
):
    row_count = queries.shape[0]
    kv_heads = keys.shape[1] // HEAD_SIZE
    q_heads = queries.shape[1] // HEAD_SIZE
    query_group_width = q_heads // kv_heads
    block_len = row_count // BLOCKS_DEV
    score_scale = 1.0 / math.sqrt(HEAD_SIZE)
    cycle_size = lax.axis_size("ctx")
    own_index = lax.axis_index("ctx")
    grad_heads = lax.all_to_all(out_grad, "tp", split_axis=1, concat_axis=0, tiled=True)
    cosine_table, sine_lookup = rope_tables(position_ids, HEAD_SIZE)
    q_flat = apply_rotation(
        queries.astype(jnp.float32).reshape(row_count, q_heads, HEAD_SIZE),
        cosine_table,
        sine_lookup,
    ).astype(jnp.bfloat16)
    q_rot = heads_first(q_flat.reshape(row_count, q_heads * HEAD_SIZE), kv_heads, query_group_width)
    rotated_keys = apply_rotation(
        keys.astype(jnp.float32).reshape(row_count, kv_heads, HEAD_SIZE), cosine_table, sine_lookup
    ).astype(jnp.bfloat16)
    value_heads = values.reshape(row_count, kv_heads, HEAD_SIZE).transpose(1, 0, 2)
    d_heads = heads_first(grad_heads, kv_heads, query_group_width)
    delta_rows = jnp.sum(
        grad_heads.astype(jnp.float32).reshape(row_count, q_heads, HEAD_SIZE)
        * attn_out.astype(jnp.float32).reshape(row_count, q_heads, HEAD_SIZE),
        axis=-1,
    )
    delta_rows = delta_rows.T.reshape(kv_heads, query_group_width, row_count)
    lse_rows = logsumexp.reshape(kv_heads, query_group_width, row_count)
    kv_pair = jnp.stack([rotated_keys.transpose(1, 0, 2), value_heads])
    every_block = jnp.arange(block_map.shape[0], dtype=jnp.int32)
    inside = (every_block[:, None] >= span_blocks[None, :, 0]) & (
        every_block[:, None] < span_blocks[None, :, 1]
    )
    numbers = jnp.arange(span_blocks.shape[0], dtype=jnp.int32)[None, :] + 1
    block_span = jnp.sum(jnp.where(inside, numbers, 0), axis=1) - 1

    def token_info(owner):
        seq_blocks = lax.dynamic_slice_in_dim(block_map, owner * BLOCKS_DEV, BLOCKS_DEV)
        matched = seq_blocks[:, None] == every_block[None, :]
        spans_of = jnp.sum(jnp.where(matched, block_span[None, :], 0), axis=1)
        positions = (
            seq_blocks[:, None] * block_len + jnp.arange(block_len, dtype=jnp.int32)[None, :]
        ).reshape(row_count)
        row_spans = jnp.repeat(spans_of, block_len)
        return (seq_blocks, spans_of, positions, row_spans)

    mine = token_info(own_index)

    def visit_block(dq_total, grads_total, pair_now, owner):
        my_blocks, my_spans, my_pos, my_row_spans = mine
        their_blocks, their_spans, their_pos, their_row_spans = token_info(owner)
        block_shared = (my_spans[:, None] == their_spans[None, :]) & (my_spans[:, None] >= 0)
        is_live = jnp.any((their_blocks[None, :] <= my_blocks[:, None]) | block_shared)
        k_part = pair_now[0]
        v_part = pair_now[1]

        def compute(unused):
            shared = (my_row_spans[:, None] == their_row_spans[None, :]) & (
                my_row_spans[:, None] >= 0
            )
            allowed = (their_pos[None, :] <= my_pos[:, None]) | shared
            scores = (
                jnp.einsum("kgqd,kcd->kgqc", q_rot, k_part, preferred_element_type=jnp.float32)
                * score_scale
            )
            attn_probs = jnp.exp(jnp.where(allowed, scores - lse_rows[..., None], -jnp.inf))
            value_grad = jnp.einsum(
                "kgqc,kgqd->kcd",
                attn_probs.astype(jnp.bfloat16),
                d_heads,
                preferred_element_type=jnp.float32,
            )
            grad_p = jnp.einsum(
                "kgqd,kcd->kgqc", d_heads, v_part, preferred_element_type=jnp.float32
            )
            grad_s = (attn_probs * (grad_p - delta_rows[..., None])).astype(jnp.bfloat16)
            query_grad = jnp.einsum(
                "kgqc,kcd->kgqd", grad_s, k_part, preferred_element_type=jnp.float32
            )
            key_grad = jnp.einsum(
                "kgqc,kgqd->kcd", grad_s, q_rot, preferred_element_type=jnp.float32
            )
            return (dq_total + query_grad, grads_total + jnp.stack([key_grad, value_grad]))

        def nothing(unused):
            return (dq_total, grads_total)

        return lax.cond(is_live, compute, nothing, 0)

    zero_q = jnp.zeros((kv_heads, query_group_width, row_count, HEAD_SIZE), jnp.float32)
    zero_kv = jnp.zeros((2, kv_heads, row_count, HEAD_SIZE), jnp.float32)
    dq_total, local_grads = visit_block(zero_q, zero_kv, kv_pair, own_index)

    def advance(offset, loop_state):
        pair_now, grads_now, dq_now = loop_state
        pair_now = passed_along(pair_now, "ctx", 1)
        grads_now = passed_along(grads_now, "ctx", 1)
        dq_now, grads_now = visit_block(
            dq_now, grads_now, pair_now, (own_index - offset) % cycle_size
        )
        return (pair_now, grads_now, dq_now)

    pair_end, grads_end, dq_total = lax.fori_loop(
        1, cycle_size, advance, (kv_pair, local_grads, dq_total)
    )
    grads_total = passed_along(grads_end, "ctx", 1)
    dq_rot = (dq_total * score_scale).transpose(2, 0, 1, 3).reshape(row_count, q_heads, HEAD_SIZE)
    grad_q = (
        reverse_rotation(dq_rot, cosine_table, sine_lookup)
        .astype(jnp.bfloat16)
        .reshape(row_count, q_heads * HEAD_SIZE)
    )
    rotated_key_gradient = (grads_total[0] * score_scale).transpose(1, 0, 2)
    key_gradient = (
        reverse_rotation(rotated_key_gradient, cosine_table, sine_lookup)
        .astype(jnp.bfloat16)
        .reshape(row_count, kv_heads * HEAD_SIZE)
    )
    value_gradient = (
        grads_total[1]
        .transpose(1, 0, 2)
        .astype(jnp.bfloat16)
        .reshape(row_count, kv_heads * HEAD_SIZE)
    )
    return (grad_q, key_gradient, value_gradient)


def solution(mesh):
    return jax.shard_map(
        shards,
        mesh=mesh,
        in_specs=(
            P("ctx", "tp"),
            P("ctx", "tp"),
            P("ctx", "tp"),
            P("ctx", "tp"),
            P(("ctx", "tp"), None),
            P("tp", "ctx"),
            P(None, "ctx"),
            P(),
            P(),
        ),
        out_specs=(P("ctx", "tp"), P("ctx", "tp"), P("ctx", "tp")),
        check_vma=False,
    )
```

profile of v0, /device:TPU:134, one launch (start us, length us, event | category | flops | bytes accessed | tf_op | source)
XLA Modules:
  0.0 865.0 jit_solution(15465749792115402724)
XLA Ops:
  2.3 5.9 all-to-all-start
  17.8 835.6 %while.21 = (s32[]{:T(128)}, bf16[2,1,128,128]{3,2,1,0:T(8,128)(2,1)S(1)}, f32[2,1,128,128]{3,2,1,0:T(8,128)S(1)}, f32[1,8,128,128]{3,2,1,0:T(8,128)S(1)}, s32[]...) while((s32[]{:T(128)}, ...), condition=%wide.region_11.12_spmd.clone.clone, body=%wide.region_6.11_spmd.clone.clone.sunk | while | flops 168952992 | bytes 6311362 | solution.py:163
  49.9 5.6 collective-permute-done
  63.2 5.6 collective-permute-done
  76.4 5.6 collective-permute-done
  89.7 5.6 collective-permute-done
  102.9 5.6 collective-permute-done
  116.2 5.6 collective-permute-done
  129.5 5.6 collective-permute-done
  142.7 5.6 collective-permute-done
  156.0 5.6 collective-permute-done
  169.3 5.6 collective-permute-done
  182.5 5.6 collective-permute-done
  195.8 5.6 collective-permute-done
  209.1 5.6 collective-permute-done
  222.3 5.6 collective-permute-done
  235.6 5.6 collective-permute-done
  248.8 5.6 collective-permute-done
  262.1 5.6 collective-permute-done
  275.4 5.6 collective-permute-done
  288.6 5.6 collective-permute-done
  301.9 5.6 collective-permute-done
  315.2 5.6 collective-permute-done
  328.4 5.6 collective-permute-done
  341.7 5.6 collective-permute-done
  354.9 5.6 collective-permute-done
  368.2 5.6 collective-permute-done
  381.5 5.6 collective-permute-done
  394.7 5.6 collective-permute-done
  408.0 5.6 collective-permute-done
  421.3 5.6 collective-permute-done
  434.5 5.6 collective-permute-done
  447.8 5.6 collective-permute-done
  461.1 5.6 collective-permute-done
  474.3 5.6 collective-permute-done
  487.6 5.6 collective-permute-done
  500.8 5.6 collective-permute-done
  514.1 5.6 collective-permute-done
  527.4 5.6 collective-permute-done
  540.6 5.6 collective-permute-done
  553.9 5.6 collective-permute-done
  567.2 5.6 collective-permute-done
  580.4 5.6 collective-permute-done
  593.7 5.6 collective-permute-done
  606.9 5.6 collective-permute-done
  620.2 5.6 collective-permute-done
  633.5 5.6 collective-permute-done
  646.7 5.6 collective-permute-done
  660.0 5.6 collective-permute-done
  673.3 5.6 collective-permute-done
  686.5 5.6 collective-permute-done
  699.8 5.6 collective-permute-done
  713.1 5.6 collective-permute-done
  726.3 5.6 collective-permute-done
  739.6 5.6 collective-permute-done
  752.8 5.6 collective-permute-done
  766.1 5.6 collective-permute-done
  779.4 5.6 collective-permute-done
  792.6 5.6 collective-permute-done
  805.9 5.6 collective-permute-done
  819.2 5.6 collective-permute-done
  832.4 5.6 collective-permute-done
  845.7 5.6 collective-permute-done
  857.1 6.4 collective-permute-done.2
  (1778 shorter events, 589.4 us)
Async XLA Ops:
  2.3 12.5 %all-to-all-start = ((bf16[16,8,1024]{2,0,1:T(8,128)(2,1)}), bf16[16,8,1024]{2,0,1:T(8,128)(2,1)S(1)}, u32[]{:S(2)}, u32[]{:S(2)}) async-start(bf16[16,8,1024]{2,0,1:T(8,128)(2,1)} %bitcast.149), calls=%async_computation | async-start | bytes 524288 | tf_op jit(solution)/shard_map/all_to_all | solution.py:69
  17.9 11.1 %collective-permute-start.1 = (f32[2,1,128,128]{3,2,1,0:T(8,128)S(1)}, f32[2,1,128,128]{3,2,1,0:T(8,128)S(1)}, u32[]{:S(2)}, u32[]{:S(2)}) collective-permute-start(f32[2,1,128,128]{3,2,1,0:T(8,128)S(1)} %get-tuple-element.822), channel_id=1, source_target_pairs={{504,0},{0,8},{8,16},{16,24},{24,32},{32,40},{40,48},{48,56},{56,6... | collective-permute-start | bytes 393224 | tf_op jit(solution)/shard_map/while/body/eval_jaxpr/ppermute | solution.py:18
  31.1 11.1 %collective-permute-start.1 = (f32[2,1,128,128]{3,2,1,0:T(8,128)S(1)}, f32[2,1,128,128]{3,2,1,0:T(8,128)S(1)}, u32[]{:S(2)}, u32[]{:S(2)}) collective-permute-start(f32[2,1,128,128]{3,2,1,0:T(8,128)S(1)} %get-tuple-element.822), channel_id=1, source_target_pairs={{504,0},{0,8},{8,16},{16,24},{24,32},{32,40},{40,48},{48,56},{56,6... | collective-permute-start | bytes 393224 | tf_op jit(solution)/shard_map/while/body/eval_jaxpr/ppermute | solution.py:18
  44.4 11.1 %collective-permute-start.1 = (f32[2,1,128,128]{3,2,1,0:T(8,128)S(1)}, f32[2,1,128,128]{3,2,1,0:T(8,128)S(1)}, u32[]{:S(2)}, u32[]{:S(2)}) collective-permute-start(f32[2,1,128,128]{3,2,1,0:T(8,128)S(1)} %get-tuple-element.822), channel_id=1, source_target_pairs={{504,0},{0,8},{8,16},{16,24},{24,32},{32,40},{40,48},{48,56},{56,6... | collective-permute-start | bytes 393224 | tf_op jit(solution)/shard_map/while/body/eval_jaxpr/ppermute | solution.py:18
  57.6 11.1 %collective-permute-start.1 = (f32[2,1,128,128]{3,2,1,0:T(8,128)S(1)}, f32[2,1,128,128]{3,2,1,0:T(8,128)S(1)}, u32[]{:S(2)}, u32[]{:S(2)}) collective-permute-start(f32[2,1,128,128]{3,2,1,0:T(8,128)S(1)} %get-tuple-element.822), channel_id=1, source_target_pairs={{504,0},{0,8},{8,16},{16,24},{24,32},{32,40},{40,48},{48,56},{56,6... | collective-permute-start | bytes 393224 | tf_op jit(solution)/shard_map/while/body/eval_jaxpr/ppermute | solution.py:18
  70.9 11.1 %collective-permute-start.1 = (f32[2,1,128,128]{3,2,1,0:T(8,128)S(1)}, f32[2,1,128,128]{3,2,1,0:T(8,128)S(1)}, u32[]{:S(2)}, u32[]{:S(2)}) collective-permute-start(f32[2,1,128,128]{3,2,1,0:T(8,128)S(1)} %get-tuple-element.822), channel_id=1, source_target_pairs={{504,0},{0,8},{8,16},{16,24},{24,32},{32,40},{40,48},{48,56},{56,6... | collective-permute-start | bytes 393224 | tf_op jit(solution)/shard_map/while/body/eval_jaxpr/ppermute | solution.py:18
  84.2 11.1 %collective-permute-start.1 = (f32[2,1,128,128]{3,2,1,0:T(8,128)S(1)}, f32[2,1,128,128]{3,2,1,0:T(8,128)S(1)}, u32[]{:S(2)}, u32[]{:S(2)}) collective-permute-start(f32[2,1,128,128]{3,2,1,0:T(8,128)S(1)} %get-tuple-element.822), channel_id=1, source_target_pairs={{504,0},{0,8},{8,16},{16,24},{24,32},{32,40},{40,48},{48,56},{56,6... | collective-permute-start | bytes 393224 | tf_op jit(solution)/shard_map/while/body/eval_jaxpr/ppermute | solution.py:18
  97.4 11.1 %collective-permute-start.1 = (f32[2,1,128,128]{3,2,1,0:T(8,128)S(1)}, f32[2,1,128,128]{3,2,1,0:T(8,128)S(1)}, u32[]{:S(2)}, u32[]{:S(2)}) collective-permute-start(f32[2,1,128,128]{3,2,1,0:T(8,128)S(1)} %get-tuple-element.822), channel_id=1, source_target_pairs={{504,0},{0,8},{8,16},{16,24},{24,32},{32,40},{40,48},{48,56},{56,6... | collective-permute-start | bytes 393224 | tf_op jit(solution)/shard_map/while/body/eval_jaxpr/ppermute | solution.py:18
  110.7 11.1 %collective-permute-start.1 = (f32[2,1,128,128]{3,2,1,0:T(8,128)S(1)}, f32[2,1,128,128]{3,2,1,0:T(8,128)S(1)}, u32[]{:S(2)}, u32[]{:S(2)}) collective-permute-start(f32[2,1,128,128]{3,2,1,0:T(8,128)S(1)} %get-tuple-element.822), channel_id=1, source_target_pairs={{504,0},{0,8},{8,16},{16,24},{24,32},{32,40},{40,48},{48,56},{56,6... | collective-permute-start | bytes 393224 | tf_op jit(solution)/shard_map/while/body/eval_jaxpr/ppermute | solution.py:18
  124.0 11.1 %collective-permute-start.1 = (f32[2,1,128,128]{3,2,1,0:T(8,128)S(1)}, f32[2,1,128,128]{3,2,1,0:T(8,128)S(1)}, u32[]{:S(2)}, u32[]{:S(2)}) collective-permute-start(f32[2,1,128,128]{3,2,1,0:T(8,128)S(1)} %get-tuple-element.822), channel_id=1, source_target_pairs={{504,0},{0,8},{8,16},{16,24},{24,32},{32,40},{40,48},{48,56},{56,6... | collective-permute-start | bytes 393224 | tf_op jit(solution)/shard_map/while/body/eval_jaxpr/ppermute | solution.py:18
  137.2 11.1 %collective-permute-start.1 = (f32[2,1,128,128]{3,2,1,0:T(8,128)S(1)}, f32[2,1,128,128]{3,2,1,0:T(8,128)S(1)}, u32[]{:S(2)}, u32[]{:S(2)}) collective-permute-start(f32[2,1,128,128]{3,2,1,0:T(8,128)S(1)} %get-tuple-element.822), channel_id=1, source_target_pairs={{504,0},{0,8},{8,16},{16,24},{24,32},{32,40},{40,48},{48,56},{56,6... | collective-permute-start | bytes 393224 | tf_op jit(solution)/shard_map/while/body/eval_jaxpr/ppermute | solution.py:18
  150.5 11.1 %collective-permute-start.1 = (f32[2,1,128,128]{3,2,1,0:T(8,128)S(1)}, f32[2,1,128,128]{3,2,1,0:T(8,128)S(1)}, u32[]{:S(2)}, u32[]{:S(2)}) collective-permute-start(f32[2,1,128,128]{3,2,1,0:T(8,128)S(1)} %get-tuple-element.822), channel_id=1, source_target_pairs={{504,0},{0,8},{8,16},{16,24},{24,32},{32,40},{40,48},{48,56},{56,6... | collective-permute-start | bytes 393224 | tf_op jit(solution)/shard_map/while/body/eval_jaxpr/ppermute | solution.py:18
  163.7 11.1 %collective-permute-start.1 = (f32[2,1,128,128]{3,2,1,0:T(8,128)S(1)}, f32[2,1,128,128]{3,2,1,0:T(8,128)S(1)}, u32[]{:S(2)}, u32[]{:S(2)}) collective-permute-start(f32[2,1,128,128]{3,2,1,0:T(8,128)S(1)} %get-tuple-element.822), channel_id=1, source_target_pairs={{504,0},{0,8},{8,16},{16,24},{24,32},{32,40},{40,48},{48,56},{56,6... | collective-permute-start | bytes 393224 | tf_op jit(solution)/shard_map/while/body/eval_jaxpr/ppermute | solution.py:18
  177.0 11.1 %collective-permute-start.1 = (f32[2,1,128,128]{3,2,1,0:T(8,128)S(1)}, f32[2,1,128,128]{3,2,1,0:T(8,128)S(1)}, u32[]{:S(2)}, u32[]{:S(2)}) collective-permute-start(f32[2,1,128,128]{3,2,1,0:T(8,128)S(1)} %get-tuple-element.822), channel_id=1, source_target_pairs={{504,0},{0,8},{8,16},{16,24},{24,32},{32,40},{40,48},{48,56},{56,6... | collective-permute-start | bytes 393224 | tf_op jit(solution)/shard_map/while/body/eval_jaxpr/ppermute | solution.py:18
  190.3 11.1 %collective-permute-start.1 = (f32[2,1,128,128]{3,2,1,0:T(8,128)S(1)}, f32[2,1,128,128]{3,2,1,0:T(8,128)S(1)}, u32[]{:S(2)}, u32[]{:S(2)}) collective-permute-start(f32[2,1,128,128]{3,2,1,0:T(8,128)S(1)} %get-tuple-element.822), channel_id=1, source_target_pairs={{504,0},{0,8},{8,16},{16,24},{24,32},{32,40},{40,48},{48,56},{56,6... | collective-permute-start | bytes 393224 | tf_op jit(solution)/shard_map/while/body/eval_jaxpr/ppermute | solution.py:18
  203.5 11.1 %collective-permute-start.1 = (f32[2,1,128,128]{3,2,1,0:T(8,128)S(1)}, f32[2,1,128,128]{3,2,1,0:T(8,128)S(1)}, u32[]{:S(2)}, u32[]{:S(2)}) collective-permute-start(f32[2,1,128,128]{3,2,1,0:T(8,128)S(1)} %get-tuple-element.822), channel_id=1, source_target_pairs={{504,0},{0,8},{8,16},{16,24},{24,32},{32,40},{40,48},{48,56},{56,6... | collective-permute-start | bytes 393224 | tf_op jit(solution)/shard_map/while/body/eval_jaxpr/ppermute | solution.py:18
  216.8 11.1 %collective-permute-start.1 = (f32[2,1,128,128]{3,2,1,0:T(8,128)S(1)}, f32[2,1,128,128]{3,2,1,0:T(8,128)S(1)}, u32[]{:S(2)}, u32[]{:S(2)}) collective-permute-start(f32[2,1,128,128]{3,2,1,0:T(8,128)S(1)} %get-tuple-element.822), channel_id=1, source_target_pairs={{504,0},{0,8},{8,16},{16,24},{24,32},{32,40},{40,48},{48,56},{56,6... | collective-permute-start | bytes 393224 | tf_op jit(solution)/shard_map/while/body/eval_jaxpr/ppermute | solution.py:18
  230.1 11.1 %collective-permute-start.1 = (f32[2,1,128,128]{3,2,1,0:T(8,128)S(1)}, f32[2,1,128,128]{3,2,1,0:T(8,128)S(1)}, u32[]{:S(2)}, u32[]{:S(2)}) collective-permute-start(f32[2,1,128,128]{3,2,1,0:T(8,128)S(1)} %get-tuple-element.822), channel_id=1, source_target_pairs={{504,0},{0,8},{8,16},{16,24},{24,32},{32,40},{40,48},{48,56},{56,6... | collective-permute-start | bytes 393224 | tf_op jit(solution)/shard_map/while/body/eval_jaxpr/ppermute | solution.py:18
  243.3 11.1 %collective-permute-start.1 = (f32[2,1,128,128]{3,2,1,0:T(8,128)S(1)}, f32[2,1,128,128]{3,2,1,0:T(8,128)S(1)}, u32[]{:S(2)}, u32[]{:S(2)}) collective-permute-start(f32[2,1,128,128]{3,2,1,0:T(8,128)S(1)} %get-tuple-element.822), channel_id=1, source_target_pairs={{504,0},{0,8},{8,16},{16,24},{24,32},{32,40},{40,48},{48,56},{56,6... | collective-permute-start | bytes 393224 | tf_op jit(solution)/shard_map/while/body/eval_jaxpr/ppermute | solution.py:18
  256.6 11.1 %collective-permute-start.1 = (f32[2,1,128,128]{3,2,1,0:T(8,128)S(1)}, f32[2,1,128,128]{3,2,1,0:T(8,128)S(1)}, u32[]{:S(2)}, u32[]{:S(2)}) collective-permute-start(f32[2,1,128,128]{3,2,1,0:T(8,128)S(1)} %get-tuple-element.822), channel_id=1, source_target_pairs={{504,0},{0,8},{8,16},{16,24},{24,32},{32,40},{40,48},{48,56},{56,6... | collective-permute-start | bytes 393224 | tf_op jit(solution)/shard_map/while/body/eval_jaxpr/ppermute | solution.py:18
  269.8 11.1 %collective-permute-start.1 = (f32[2,1,128,128]{3,2,1,0:T(8,128)S(1)}, f32[2,1,128,128]{3,2,1,0:T(8,128)S(1)}, u32[]{:S(2)}, u32[]{:S(2)}) collective-permute-start(f32[2,1,128,128]{3,2,1,0:T(8,128)S(1)} %get-tuple-element.822), channel_id=1, source_target_pairs={{504,0},{0,8},{8,16},{16,24},{24,32},{32,40},{40,48},{48,56},{56,6... | collective-permute-start | bytes 393224 | tf_op jit(solution)/shard_map/while/body/eval_jaxpr/ppermute | solution.py:18
  283.1 11.1 %collective-permute-start.1 = (f32[2,1,128,128]{3,2,1,0:T(8,128)S(1)}, f32[2,1,128,128]{3,2,1,0:T(8,128)S(1)}, u32[]{:S(2)}, u32[]{:S(2)}) collective-permute-start(f32[2,1,128,128]{3,2,1,0:T(8,128)S(1)} %get-tuple-element.822), channel_id=1, source_target_pairs={{504,0},{0,8},{8,16},{16,24},{24,32},{32,40},{40,48},{48,56},{56,6... | collective-permute-start | bytes 393224 | tf_op jit(solution)/shard_map/while/body/eval_jaxpr/ppermute | solution.py:18
  296.4 11.1 %collective-permute-start.1 = (f32[2,1,128,128]{3,2,1,0:T(8,128)S(1)}, f32[2,1,128,128]{3,2,1,0:T(8,128)S(1)}, u32[]{:S(2)}, u32[]{:S(2)}) collective-permute-start(f32[2,1,128,128]{3,2,1,0:T(8,128)S(1)} %get-tuple-element.822), channel_id=1, source_target_pairs={{504,0},{0,8},{8,16},{16,24},{24,32},{32,40},{40,48},{48,56},{56,6... | collective-permute-start | bytes 393224 | tf_op jit(solution)/shard_map/while/body/eval_jaxpr/ppermute | solution.py:18
  309.6 11.1 %collective-permute-start.1 = (f32[2,1,128,128]{3,2,1,0:T(8,128)S(1)}, f32[2,1,128,128]{3,2,1,0:T(8,128)S(1)}, u32[]{:S(2)}, u32[]{:S(2)}) collective-permute-start(f32[2,1,128,128]{3,2,1,0:T(8,128)S(1)} %get-tuple-element.822), channel_id=1, source_target_pairs={{504,0},{0,8},{8,16},{16,24},{24,32},{32,40},{40,48},{48,56},{56,6... | collective-permute-start | bytes 393224 | tf_op jit(solution)/shard_map/while/body/eval_jaxpr/ppermute | solution.py:18
  322.9 11.1 %collective-permute-start.1 = (f32[2,1,128,128]{3,2,1,0:T(8,128)S(1)}, f32[2,1,128,128]{3,2,1,0:T(8,128)S(1)}, u32[]{:S(2)}, u32[]{:S(2)}) collective-permute-start(f32[2,1,128,128]{3,2,1,0:T(8,128)S(1)} %get-tuple-element.822), channel_id=1, source_target_pairs={{504,0},{0,8},{8,16},{16,24},{24,32},{32,40},{40,48},{48,56},{56,6... | collective-permute-start | bytes 393224 | tf_op jit(solution)/shard_map/while/body/eval_jaxpr/ppermute | solution.py:18
  336.2 11.1 %collective-permute-start.1 = (f32[2,1,128,128]{3,2,1,0:T(8,128)S(1)}, f32[2,1,128,128]{3,2,1,0:T(8,128)S(1)}, u32[]{:S(2)}, u32[]{:S(2)}) collective-permute-start(f32[2,1,128,128]{3,2,1,0:T(8,128)S(1)} %get-tuple-element.822), channel_id=1, source_target_pairs={{504,0},{0,8},{8,16},{16,24},{24,32},{32,40},{40,48},{48,56},{56,6... | collective-permute-start | bytes 393224 | tf_op jit(solution)/shard_map/while/body/eval_jaxpr/ppermute | solution.py:18
  349.4 11.1 %collective-permute-start.1 = (f32[2,1,128,128]{3,2,1,0:T(8,128)S(1)}, f32[2,1,128,128]{3,2,1,0:T(8,128)S(1)}, u32[]{:S(2)}, u32[]{:S(2)}) collective-permute-start(f32[2,1,128,128]{3,2,1,0:T(8,128)S(1)} %get-tuple-element.822), channel_id=1, source_target_pairs={{504,0},{0,8},{8,16},{16,24},{24,32},{32,40},{40,48},{48,56},{56,6... | collective-permute-start | bytes 393224 | tf_op jit(solution)/shard_map/while/body/eval_jaxpr/ppermute | solution.py:18
  362.7 11.1 %collective-permute-start.1 = (f32[2,1,128,128]{3,2,1,0:T(8,128)S(1)}, f32[2,1,128,128]{3,2,1,0:T(8,128)S(1)}, u32[]{:S(2)}, u32[]{:S(2)}) collective-permute-start(f32[2,1,128,128]{3,2,1,0:T(8,128)S(1)} %get-tuple-element.822), channel_id=1, source_target_pairs={{504,0},{0,8},{8,16},{16,24},{24,32},{32,40},{40,48},{48,56},{56,6... | collective-permute-start | bytes 393224 | tf_op jit(solution)/shard_map/while/body/eval_jaxpr/ppermute | solution.py:18
  376.0 11.1 %collective-permute-start.1 = (f32[2,1,128,128]{3,2,1,0:T(8,128)S(1)}, f32[2,1,128,128]{3,2,1,0:T(8,128)S(1)}, u32[]{:S(2)}, u32[]{:S(2)}) collective-permute-start(f32[2,1,128,128]{3,2,1,0:T(8,128)S(1)} %get-tuple-element.822), channel_id=1, source_target_pairs={{504,0},{0,8},{8,16},{16,24},{24,32},{32,40},{40,48},{48,56},{56,6... | collective-permute-start | bytes 393224 | tf_op jit(solution)/shard_map/while/body/eval_jaxpr/ppermute | solution.py:18
  389.2 11.1 %collective-permute-start.1 = (f32[2,1,128,128]{3,2,1,0:T(8,128)S(1)}, f32[2,1,128,128]{3,2,1,0:T(8,128)S(1)}, u32[]{:S(2)}, u32[]{:S(2)}) collective-permute-start(f32[2,1,128,128]{3,2,1,0:T(8,128)S(1)} %get-tuple-element.822), channel_id=1, source_target_pairs={{504,0},{0,8},{8,16},{16,24},{24,32},{32,40},{40,48},{48,56},{56,6... | collective-permute-start | bytes 393224 | tf_op jit(solution)/shard_map/while/body/eval_jaxpr/ppermute | solution.py:18
  402.5 11.1 %collective-permute-start.1 = (f32[2,1,128,128]{3,2,1,0:T(8,128)S(1)}, f32[2,1,128,128]{3,2,1,0:T(8,128)S(1)}, u32[]{:S(2)}, u32[]{:S(2)}) collective-permute-start(f32[2,1,128,128]{3,2,1,0:T(8,128)S(1)} %get-tuple-element.822), channel_id=1, source_target_pairs={{504,0},{0,8},{8,16},{16,24},{24,32},{32,40},{40,48},{48,56},{56,6... | collective-permute-start | bytes 393224 | tf_op jit(solution)/shard_map/while/body/eval_jaxpr/ppermute | solution.py:18
  415.7 11.1 %collective-permute-start.1 = (f32[2,1,128,128]{3,2,1,0:T(8,128)S(1)}, f32[2,1,128,128]{3,2,1,0:T(8,128)S(1)}, u32[]{:S(2)}, u32[]{:S(2)}) collective-permute-start(f32[2,1,128,128]{3,2,1,0:T(8,128)S(1)} %get-tuple-element.822), channel_id=1, source_target_pairs={{504,0},{0,8},{8,16},{16,24},{24,32},{32,40},{40,48},{48,56},{56,6... | collective-permute-start | bytes 393224 | tf_op jit(solution)/shard_map/while/body/eval_jaxpr/ppermute | solution.py:18
  429.0 11.1 %collective-permute-start.1 = (f32[2,1,128,128]{3,2,1,0:T(8,128)S(1)}, f32[2,1,128,128]{3,2,1,0:T(8,128)S(1)}, u32[]{:S(2)}, u32[]{:S(2)}) collective-permute-start(f32[2,1,128,128]{3,2,1,0:T(8,128)S(1)} %get-tuple-element.822), channel_id=1, source_target_pairs={{504,0},{0,8},{8,16},{16,24},{24,32},{32,40},{40,48},{48,56},{56,6... | collective-permute-start | bytes 393224 | tf_op jit(solution)/shard_map/while/body/eval_jaxpr/ppermute | solution.py:18
  442.3 11.1 %collective-permute-start.1 = (f32[2,1,128,128]{3,2,1,0:T(8,128)S(1)}, f32[2,1,128,128]{3,2,1,0:T(8,128)S(1)}, u32[]{:S(2)}, u32[]{:S(2)}) collective-permute-start(f32[2,1,128,128]{3,2,1,0:T(8,128)S(1)} %get-tuple-element.822), channel_id=1, source_target_pairs={{504,0},{0,8},{8,16},{16,24},{24,32},{32,40},{40,48},{48,56},{56,6... | collective-permute-start | bytes 393224 | tf_op jit(solution)/shard_map/while/body/eval_jaxpr/ppermute | solution.py:18
  455.5 11.1 %collective-permute-start.1 = (f32[2,1,128,128]{3,2,1,0:T(8,128)S(1)}, f32[2,1,128,128]{3,2,1,0:T(8,128)S(1)}, u32[]{:S(2)}, u32[]{:S(2)}) collective-permute-start(f32[2,1,128,128]{3,2,1,0:T(8,128)S(1)} %get-tuple-element.822), channel_id=1, source_target_pairs={{504,0},{0,8},{8,16},{16,24},{24,32},{32,40},{40,48},{48,56},{56,6... | collective-permute-start | bytes 393224 | tf_op jit(solution)/shard_map/while/body/eval_jaxpr/ppermute | solution.py:18
  468.8 11.1 %collective-permute-start.1 = (f32[2,1,128,128]{3,2,1,0:T(8,128)S(1)}, f32[2,1,128,128]{3,2,1,0:T(8,128)S(1)}, u32[]{:S(2)}, u32[]{:S(2)}) collective-permute-start(f32[2,1,128,128]{3,2,1,0:T(8,128)S(1)} %get-tuple-element.822), channel_id=1, source_target_pairs={{504,0},{0,8},{8,16},{16,24},{24,32},{32,40},{40,48},{48,56},{56,6... | collective-permute-start | bytes 393224 | tf_op jit(solution)/shard_map/while/body/eval_jaxpr/ppermute | solution.py:18
  482.1 11.1 %collective-permute-start.1 = (f32[2,1,128,128]{3,2,1,0:T(8,128)S(1)}, f32[2,1,128,128]{3,2,1,0:T(8,128)S(1)}, u32[]{:S(2)}, u32[]{:S(2)}) collective-permute-start(f32[2,1,128,128]{3,2,1,0:T(8,128)S(1)} %get-tuple-element.822), channel_id=1, source_target_pairs={{504,0},{0,8},{8,16},{16,24},{24,32},{32,40},{40,48},{48,56},{56,6... | collective-permute-start | bytes 393224 | tf_op jit(solution)/shard_map/while/body/eval_jaxpr/ppermute | solution.py:18
  495.3 11.1 %collective-permute-start.1 = (f32[2,1,128,128]{3,2,1,0:T(8,128)S(1)}, f32[2,1,128,128]{3,2,1,0:T(8,128)S(1)}, u32[]{:S(2)}, u32[]{:S(2)}) collective-permute-start(f32[2,1,128,128]{3,2,1,0:T(8,128)S(1)} %get-tuple-element.822), channel_id=1, source_target_pairs={{504,0},{0,8},{8,16},{16,24},{24,32},{32,40},{40,48},{48,56},{56,6... | collective-permute-start | bytes 393224 | tf_op jit(solution)/shard_map/while/body/eval_jaxpr/ppermute | solution.py:18
  508.6 11.1 %collective-permute-start.1 = (f32[2,1,128,128]{3,2,1,0:T(8,128)S(1)}, f32[2,1,128,128]{3,2,1,0:T(8,128)S(1)}, u32[]{:S(2)}, u32[]{:S(2)}) collective-permute-start(f32[2,1,128,128]{3,2,1,0:T(8,128)S(1)} %get-tuple-element.822), channel_id=1, source_target_pairs={{504,0},{0,8},{8,16},{16,24},{24,32},{32,40},{40,48},{48,56},{56,6... | collective-permute-start | bytes 393224 | tf_op jit(solution)/shard_map/while/body/eval_jaxpr/ppermute | solution.py:18
  521.8 11.1 %collective-permute-start.1 = (f32[2,1,128,128]{3,2,1,0:T(8,128)S(1)}, f32[2,1,128,128]{3,2,1,0:T(8,128)S(1)}, u32[]{:S(2)}, u32[]{:S(2)}) collective-permute-start(f32[2,1,128,128]{3,2,1,0:T(8,128)S(1)} %get-tuple-element.822), channel_id=1, source_target_pairs={{504,0},{0,8},{8,16},{16,24},{24,32},{32,40},{40,48},{48,56},{56,6... | collective-permute-start | bytes 393224 | tf_op jit(solution)/shard_map/while/body/eval_jaxpr/ppermute | solution.py:18
  535.1 11.1 %collective-permute-start.1 = (f32[2,1,128,128]{3,2,1,0:T(8,128)S(1)}, f32[2,1,128,128]{3,2,1,0:T(8,128)S(1)}, u32[]{:S(2)}, u32[]{:S(2)}) collective-permute-start(f32[2,1,128,128]{3,2,1,0:T(8,128)S(1)} %get-tuple-element.822), channel_id=1, source_target_pairs={{504,0},{0,8},{8,16},{16,24},{24,32},{32,40},{40,48},{48,56},{56,6... | collective-permute-start | bytes 393224 | tf_op jit(solution)/shard_map/while/body/eval_jaxpr/ppermute | solution.py:18
  548.4 11.1 %collective-permute-start.1 = (f32[2,1,128,128]{3,2,1,0:T(8,128)S(1)}, f32[2,1,128,128]{3,2,1,0:T(8,128)S(1)}, u32[]{:S(2)}, u32[]{:S(2)}) collective-permute-start(f32[2,1,128,128]{3,2,1,0:T(8,128)S(1)} %get-tuple-element.822), channel_id=1, source_target_pairs={{504,0},{0,8},{8,16},{16,24},{24,32},{32,40},{40,48},{48,56},{56,6... | collective-permute-start | bytes 393224 | tf_op jit(solution)/shard_map/while/body/eval_jaxpr/ppermute | solution.py:18
  561.6 11.1 %collective-permute-start.1 = (f32[2,1,128,128]{3,2,1,0:T(8,128)S(1)}, f32[2,1,128,128]{3,2,1,0:T(8,128)S(1)}, u32[]{:S(2)}, u32[]{:S(2)}) collective-permute-start(f32[2,1,128,128]{3,2,1,0:T(8,128)S(1)} %get-tuple-element.822), channel_id=1, source_target_pairs={{504,0},{0,8},{8,16},{16,24},{24,32},{32,40},{40,48},{48,56},{56,6... | collective-permute-start | bytes 393224 | tf_op jit(solution)/shard_map/while/body/eval_jaxpr/ppermute | solution.py:18
  574.9 11.1 %collective-permute-start.1 = (f32[2,1,128,128]{3,2,1,0:T(8,128)S(1)}, f32[2,1,128,128]{3,2,1,0:T(8,128)S(1)}, u32[]{:S(2)}, u32[]{:S(2)}) collective-permute-start(f32[2,1,128,128]{3,2,1,0:T(8,128)S(1)} %get-tuple-element.822), channel_id=1, source_target_pairs={{504,0},{0,8},{8,16},{16,24},{24,32},{32,40},{40,48},{48,56},{56,6... | collective-permute-start | bytes 393224 | tf_op jit(solution)/shard_map/while/body/eval_jaxpr/ppermute | solution.py:18
  588.2 11.1 %collective-permute-start.1 = (f32[2,1,128,128]{3,2,1,0:T(8,128)S(1)}, f32[2,1,128,128]{3,2,1,0:T(8,128)S(1)}, u32[]{:S(2)}, u32[]{:S(2)}) collective-permute-start(f32[2,1,128,128]{3,2,1,0:T(8,128)S(1)} %get-tuple-element.822), channel_id=1, source_target_pairs={{504,0},{0,8},{8,16},{16,24},{24,32},{32,40},{40,48},{48,56},{56,6... | collective-permute-start | bytes 393224 | tf_op jit(solution)/shard_map/while/body/eval_jaxpr/ppermute | solution.py:18
  601.4 11.1 %collective-permute-start.1 = (f32[2,1,128,128]{3,2,1,0:T(8,128)S(1)}, f32[2,1,128,128]{3,2,1,0:T(8,128)S(1)}, u32[]{:S(2)}, u32[]{:S(2)}) collective-permute-start(f32[2,1,128,128]{3,2,1,0:T(8,128)S(1)} %get-tuple-element.822), channel_id=1, source_target_pairs={{504,0},{0,8},{8,16},{16,24},{24,32},{32,40},{40,48},{48,56},{56,6... | collective-permute-start | bytes 393224 | tf_op jit(solution)/shard_map/while/body/eval_jaxpr/ppermute | solution.py:18
  614.7 11.1 %collective-permute-start.1 = (f32[2,1,128,128]{3,2,1,0:T(8,128)S(1)}, f32[2,1,128,128]{3,2,1,0:T(8,128)S(1)}, u32[]{:S(2)}, u32[]{:S(2)}) collective-permute-start(f32[2,1,128,128]{3,2,1,0:T(8,128)S(1)} %get-tuple-element.822), channel_id=1, source_target_pairs={{504,0},{0,8},{8,16},{16,24},{24,32},{32,40},{40,48},{48,56},{56,6... | collective-permute-start | bytes 393224 | tf_op jit(solution)/shard_map/while/body/eval_jaxpr/ppermute | solution.py:18
  628.0 11.1 %collective-permute-start.1 = (f32[2,1,128,128]{3,2,1,0:T(8,128)S(1)}, f32[2,1,128,128]{3,2,1,0:T(8,128)S(1)}, u32[]{:S(2)}, u32[]{:S(2)}) collective-permute-start(f32[2,1,128,128]{3,2,1,0:T(8,128)S(1)} %get-tuple-element.822), channel_id=1, source_target_pairs={{504,0},{0,8},{8,16},{16,24},{24,32},{32,40},{40,48},{48,56},{56,6... | collective-permute-start | bytes 393224 | tf_op jit(solution)/shard_map/while/body/eval_jaxpr/ppermute | solution.py:18
  641.2 11.1 %collective-permute-start.1 = (f32[2,1,128,128]{3,2,1,0:T(8,128)S(1)}, f32[2,1,128,128]{3,2,1,0:T(8,128)S(1)}, u32[]{:S(2)}, u32[]{:S(2)}) collective-permute-start(f32[2,1,128,128]{3,2,1,0:T(8,128)S(1)} %get-tuple-element.822), channel_id=1, source_target_pairs={{504,0},{0,8},{8,16},{16,24},{24,32},{32,40},{40,48},{48,56},{56,6... | collective-permute-start | bytes 393224 | tf_op jit(solution)/shard_map/while/body/eval_jaxpr/ppermute | solution.py:18
  654.5 11.1 %collective-permute-start.1 = (f32[2,1,128,128]{3,2,1,0:T(8,128)S(1)}, f32[2,1,128,128]{3,2,1,0:T(8,128)S(1)}, u32[]{:S(2)}, u32[]{:S(2)}) collective-permute-start(f32[2,1,128,128]{3,2,1,0:T(8,128)S(1)} %get-tuple-element.822), channel_id=1, source_target_pairs={{504,0},{0,8},{8,16},{16,24},{24,32},{32,40},{40,48},{48,56},{56,6... | collective-permute-start | bytes 393224 | tf_op jit(solution)/shard_map/while/body/eval_jaxpr/ppermute | solution.py:18
  667.7 11.1 %collective-permute-start.1 = (f32[2,1,128,128]{3,2,1,0:T(8,128)S(1)}, f32[2,1,128,128]{3,2,1,0:T(8,128)S(1)}, u32[]{:S(2)}, u32[]{:S(2)}) collective-permute-start(f32[2,1,128,128]{3,2,1,0:T(8,128)S(1)} %get-tuple-element.822), channel_id=1, source_target_pairs={{504,0},{0,8},{8,16},{16,24},{24,32},{32,40},{40,48},{48,56},{56,6... | collective-permute-start | bytes 393224 | tf_op jit(solution)/shard_map/while/body/eval_jaxpr/ppermute | solution.py:18
  681.0 11.1 %collective-permute-start.1 = (f32[2,1,128,128]{3,2,1,0:T(8,128)S(1)}, f32[2,1,128,128]{3,2,1,0:T(8,128)S(1)}, u32[]{:S(2)}, u32[]{:S(2)}) collective-permute-start(f32[2,1,128,128]{3,2,1,0:T(8,128)S(1)} %get-tuple-element.822), channel_id=1, source_target_pairs={{504,0},{0,8},{8,16},{16,24},{24,32},{32,40},{40,48},{48,56},{56,6... | collective-permute-start | bytes 393224 | tf_op jit(solution)/shard_map/while/body/eval_jaxpr/ppermute | solution.py:18
  694.3 11.1 %collective-permute-start.1 = (f32[2,1,128,128]{3,2,1,0:T(8,128)S(1)}, f32[2,1,128,128]{3,2,1,0:T(8,128)S(1)}, u32[]{:S(2)}, u32[]{:S(2)}) collective-permute-start(f32[2,1,128,128]{3,2,1,0:T(8,128)S(1)} %get-tuple-element.822), channel_id=1, source_target_pairs={{504,0},{0,8},{8,16},{16,24},{24,32},{32,40},{40,48},{48,56},{56,6... | collective-permute-start | bytes 393224 | tf_op jit(solution)/shard_map/while/body/eval_jaxpr/ppermute | solution.py:18
  707.5 11.1 %collective-permute-start.1 = (f32[2,1,128,128]{3,2,1,0:T(8,128)S(1)}, f32[2,1,128,128]{3,2,1,0:T(8,128)S(1)}, u32[]{:S(2)}, u32[]{:S(2)}) collective-permute-start(f32[2,1,128,128]{3,2,1,0:T(8,128)S(1)} %get-tuple-element.822), channel_id=1, source_target_pairs={{504,0},{0,8},{8,16},{16,24},{24,32},{32,40},{40,48},{48,56},{56,6... | collective-permute-start | bytes 393224 | tf_op jit(solution)/shard_map/while/body/eval_jaxpr/ppermute | solution.py:18
  720.8 11.1 %collective-permute-start.1 = (f32[2,1,128,128]{3,2,1,0:T(8,128)S(1)}, f32[2,1,128,128]{3,2,1,0:T(8,128)S(1)}, u32[]{:S(2)}, u32[]{:S(2)}) collective-permute-start(f32[2,1,128,128]{3,2,1,0:T(8,128)S(1)} %get-tuple-element.822), channel_id=1, source_target_pairs={{504,0},{0,8},{8,16},{16,24},{24,32},{32,40},{40,48},{48,56},{56,6... | collective-permute-start | bytes 393224 | tf_op jit(solution)/shard_map/while/body/eval_jaxpr/ppermute | solution.py:18
  734.1 11.1 %collective-permute-start.1 = (f32[2,1,128,128]{3,2,1,0:T(8,128)S(1)}, f32[2,1,128,128]{3,2,1,0:T(8,128)S(1)}, u32[]{:S(2)}, u32[]{:S(2)}) collective-permute-start(f32[2,1,128,128]{3,2,1,0:T(8,128)S(1)} %get-tuple-element.822), channel_id=1, source_target_pairs={{504,0},{0,8},{8,16},{16,24},{24,32},{32,40},{40,48},{48,56},{56,6... | collective-permute-start | bytes 393224 | tf_op jit(solution)/shard_map/while/body/eval_jaxpr/ppermute | solution.py:18
  747.3 11.1 %collective-permute-start.1 = (f32[2,1,128,128]{3,2,1,0:T(8,128)S(1)}, f32[2,1,128,128]{3,2,1,0:T(8,128)S(1)}, u32[]{:S(2)}, u32[]{:S(2)}) collective-permute-start(f32[2,1,128,128]{3,2,1,0:T(8,128)S(1)} %get-tuple-element.822), channel_id=1, source_target_pairs={{504,0},{0,8},{8,16},{16,24},{24,32},{32,40},{40,48},{48,56},{56,6... | collective-permute-start | bytes 393224 | tf_op jit(solution)/shard_map/while/body/eval_jaxpr/ppermute | solution.py:18
  760.6 11.1 %collective-permute-start.1 = (f32[2,1,128,128]{3,2,1,0:T(8,128)S(1)}, f32[2,1,128,128]{3,2,1,0:T(8,128)S(1)}, u32[]{:S(2)}, u32[]{:S(2)}) collective-permute-start(f32[2,1,128,128]{3,2,1,0:T(8,128)S(1)} %get-tuple-element.822), channel_id=1, source_target_pairs={{504,0},{0,8},{8,16},{16,24},{24,32},{32,40},{40,48},{48,56},{56,6... | collective-permute-start | bytes 393224 | tf_op jit(solution)/shard_map/while/body/eval_jaxpr/ppermute | solution.py:18
  773.8 11.1 %collective-permute-start.1 = (f32[2,1,128,128]{3,2,1,0:T(8,128)S(1)}, f32[2,1,128,128]{3,2,1,0:T(8,128)S(1)}, u32[]{:S(2)}, u32[]{:S(2)}) collective-permute-start(f32[2,1,128,128]{3,2,1,0:T(8,128)S(1)} %get-tuple-element.822), channel_id=1, source_target_pairs={{504,0},{0,8},{8,16},{16,24},{24,32},{32,40},{40,48},{48,56},{56,6... | collective-permute-start | bytes 393224 | tf_op jit(solution)/shard_map/while/body/eval_jaxpr/ppermute | solution.py:18
  787.1 11.1 %collective-permute-start.1 = (f32[2,1,128,128]{3,2,1,0:T(8,128)S(1)}, f32[2,1,128,128]{3,2,1,0:T(8,128)S(1)}, u32[]{:S(2)}, u32[]{:S(2)}) collective-permute-start(f32[2,1,128,128]{3,2,1,0:T(8,128)S(1)} %get-tuple-element.822), channel_id=1, source_target_pairs={{504,0},{0,8},{8,16},{16,24},{24,32},{32,40},{40,48},{48,56},{56,6... | collective-permute-start | bytes 393224 | tf_op jit(solution)/shard_map/while/body/eval_jaxpr/ppermute | solution.py:18
  800.4 11.1 %collective-permute-start.1 = (f32[2,1,128,128]{3,2,1,0:T(8,128)S(1)}, f32[2,1,128,128]{3,2,1,0:T(8,128)S(1)}, u32[]{:S(2)}, u32[]{:S(2)}) collective-permute-start(f32[2,1,128,128]{3,2,1,0:T(8,128)S(1)} %get-tuple-element.822), channel_id=1, source_target_pairs={{504,0},{0,8},{8,16},{16,24},{24,32},{32,40},{40,48},{48,56},{56,6... | collective-permute-start | bytes 393224 | tf_op jit(solution)/shard_map/while/body/eval_jaxpr/ppermute | solution.py:18
  813.6 11.1 %collective-permute-start.1 = (f32[2,1,128,128]{3,2,1,0:T(8,128)S(1)}, f32[2,1,128,128]{3,2,1,0:T(8,128)S(1)}, u32[]{:S(2)}, u32[]{:S(2)}) collective-permute-start(f32[2,1,128,128]{3,2,1,0:T(8,128)S(1)} %get-tuple-element.822), channel_id=1, source_target_pairs={{504,0},{0,8},{8,16},{16,24},{24,32},{32,40},{40,48},{48,56},{56,6... | collective-permute-start | bytes 393224 | tf_op jit(solution)/shard_map/while/body/eval_jaxpr/ppermute | solution.py:18
  826.9 11.1 %collective-permute-start.1 = (f32[2,1,128,128]{3,2,1,0:T(8,128)S(1)}, f32[2,1,128,128]{3,2,1,0:T(8,128)S(1)}, u32[]{:S(2)}, u32[]{:S(2)}) collective-permute-start(f32[2,1,128,128]{3,2,1,0:T(8,128)S(1)} %get-tuple-element.822), channel_id=1, source_target_pairs={{504,0},{0,8},{8,16},{16,24},{24,32},{32,40},{40,48},{48,56},{56,6... | collective-permute-start | bytes 393224 | tf_op jit(solution)/shard_map/while/body/eval_jaxpr/ppermute | solution.py:18
  840.2 11.1 %collective-permute-start.1 = (f32[2,1,128,128]{3,2,1,0:T(8,128)S(1)}, f32[2,1,128,128]{3,2,1,0:T(8,128)S(1)}, u32[]{:S(2)}, u32[]{:S(2)}) collective-permute-start(f32[2,1,128,128]{3,2,1,0:T(8,128)S(1)} %get-tuple-element.822), channel_id=1, source_target_pairs={{504,0},{0,8},{8,16},{16,24},{24,32},{32,40},{40,48},{48,56},{56,6... | collective-permute-start | bytes 393224 | tf_op jit(solution)/shard_map/while/body/eval_jaxpr/ppermute | solution.py:18
  (72 other events, 601.5 us)
where the time goes:
time: 870 us; the launch traced here: 865 us
  waiting for transfers between devices  356 us (41%)
  starting transfers between devices  254 us (29%)
  matrix products  82.1 us (9%)
  other arithmetic  76.1 us (9%)
  loops' own time  52.1 us (6%)
  local copies, waits for them, and re-layouts  43.5 us (5%)
    ppermute x127, waiting for transfers between devices, passed_along(): return lax.ppermute(block, axis, route)  356 us
    ppermute x127, starting transfers between devices, passed_along(): return lax.ppermute(block, axis, route)  248 us
    another operation x1, loops' own time, shards(): lax.fori_loop(1, cycle_size, advance, (kv_pair, local_grads, dq_total))  47 us
    reduce_or x64, other arithmetic, visit_block(): jnp.any((their_blocks[None, :] <= my_blocks[:, None]) | block_shared)  45.3 us
    dot_general x64, matrix products, compute(): jnp.einsum('kgqc,kgqd->kcd', attn_probs.astype(jnp.bfloat16), d_heads, pr...  17.6 us
  transfers between devices with their start and end apart: 128, of which 64 were waited for; matrix products, arithmetic and copies ran while one was open for 8% of the time, Pallas kernels for 0%

commit v1 on v0

v1 whole, which is shorter than its diff:
```python
import math

import jax
import jax.numpy as jnp
from jax import lax
from jax.experimental import pallas as pl
from jax.experimental.pallas import tpu as pltpu
from jax.sharding import PartitionSpec as P

HEAD = 128
BLK = 64
QUAD = 4
THETA = 1000000.0
LOG2E = 1.4426950408889634
TILE = 256


def rope_tables(position_ids):
    half = HEAD // 2
    pair = jnp.arange(HEAD, dtype=jnp.int32) % half
    inverse = jnp.exp(pair.astype(jnp.float32) * jnp.float32(-2.0 * math.log(THETA) / HEAD))
    first_cut = HEAD // 8
    second_cut = first_cut + 3 * HEAD // 16
    picked = jnp.where(
        pair[None, :] < first_cut,
        position_ids[0][:, None],
        jnp.where(pair[None, :] < second_cut, position_ids[1][:, None], position_ids[2][:, None]),
    )
    angles = picked.astype(jnp.float32) * inverse[None, :]
    sign = jnp.where(jnp.arange(HEAD) < half, -1.0, 1.0).astype(jnp.float32)
    return jnp.cos(angles), jnp.sin(angles) * sign[None, :]


def rotate(field, cosine, sine):
    rows, width = field.shape
    x = field.astype(jnp.float32).reshape(rows, width // HEAD, HEAD)
    out = x * cosine[:, None, :] + jnp.roll(x, HEAD // 2, axis=-1) * sine[:, None, :]
    return out.reshape(rows, width)


def plan(block_map, span_blocks, z, j):
    nz = block_map.shape[0] // (2 * QUAD)
    kseq = lax.dynamic_index_in_dim(block_map.reshape(nz, QUAD, 2), j, 1, False).reshape(-1)
    qseq = lax.dynamic_slice_in_dim(block_map, z * 2 * QUAD, 2 * QUAD)
    rank = jnp.sum(kseq[None, :] < kseq[:, None], axis=1).astype(jnp.int32)
    places = jnp.arange(kseq.shape[0], dtype=jnp.int32)
    hit = rank[None, :] == places[:, None]
    order = jnp.sum(jnp.where(hit, places[None, :], 0), axis=1)
    kseq_sorted = jnp.sum(jnp.where(hit, kseq[None, :], 0), axis=1)
    inside = (qseq[:, None] >= span_blocks[None, :, 0]) & (qseq[:, None] < span_blocks[None, :, 1])
    last = jnp.sum(jnp.where(inside, span_blocks[None, :, 1], 0), axis=1)
    limit = jnp.maximum(qseq, last - 1)
    count = jnp.sum(kseq[None, :] <= limit[:, None], axis=1).astype(jnp.int32)
    per_tile = TILE // BLK
    tiles = (count + per_tile - 1) // per_tile
    return jnp.concatenate([order, kseq_sorted, qseq * BLK, last * BLK - 1, tiles])


def attention_kernel(info, q_ref, do_ref, st_ref, kv_ref, dq_ref, dkv_ref, ks, vs, dk, dv, dqa):
    nk = kv_ref.shape[0] * 2
    nq = q_ref.shape[0] * 2
    heads = q_ref.shape[2] // HEAD
    width = heads * BLK
    scale = 1.0 / math.sqrt(HEAD)
    base = 2 * nk

    def sort(s, carry):
        source = info[s]
        chunk = source // 2
        row = pl.multiple_of((source % 2) * BLK, BLK)
        to = pl.multiple_of(s * BLK, BLK)
        ks[pl.ds(to, BLK), :] = kv_ref[chunk, 0, pl.ds(row, BLK), :]
        vs[pl.ds(to, BLK), :] = kv_ref[chunk, 1, pl.ds(row, BLK), :]
        return carry

    lax.fori_loop(0, nk, sort, 0)
    dk[...] = jnp.zeros_like(dk)
    dv[...] = jnp.zeros_like(dv)
    lane = lax.broadcasted_iota(jnp.int32, (1, width), 1) % BLK
    sub = lax.broadcasted_iota(jnp.int32, (BLK, width), 0)

    def one_block(b, carry):
        m = b // 2
        half = b % 2
        row = pl.multiple_of(half * BLK, BLK)
        q_rows = q_ref[m, pl.ds(row, BLK), :]
        do_rows = do_ref[m, pl.ds(row, BLK), :]
        qb = jnp.concatenate([q_rows[:, h * HEAD : (h + 1) * HEAD] for h in range(heads)], axis=0)
        dob = jnp.concatenate([do_rows[:, h * HEAD : (h + 1) * HEAD] for h in range(heads)], axis=0)
        lse = jnp.concatenate([st_ref[m, 0, half, k : k + 1, :] for k in range(heads // 2)], axis=1)
        delta = jnp.concatenate([st_ref[m, 1, half, k : k + 1, :] for k in range(heads // 2)], axis=1)
        limit = jnp.maximum(info[base + b] + lane, info[base + nq + b])
        dqa[...] = jnp.zeros_like(dqa)

        def one_tile(t, inner):
            at = pl.multiple_of(t * TILE, TILE)
            kt = ks[pl.ds(at, TILE), :]
            vt = vs[pl.ds(at, TILE), :]
            s = lax.dot_general(kt, qb, (((1,), (1,)), ((), ())), preferred_element_type=jnp.float32)
            dp = lax.dot_general(vt, dob, (((1,), (1,)), ((), ())), preferred_element_type=jnp.float32)
            x = s * (scale * LOG2E) - lse
            keep = jnp.concatenate(
                [sub <= limit - info[nk + t * (TILE // BLK) + i] * BLK for i in range(TILE // BLK)], axis=0
            )
            p = jnp.exp2(jnp.where(keep, x, -jnp.inf))
            ds = (p * (dp - delta)).astype(jnp.bfloat16)
            dv[pl.ds(at, TILE), :] += jnp.dot(
                p.astype(jnp.bfloat16), dob, preferred_element_type=jnp.float32
            )
            dk[pl.ds(at, TILE), :] += jnp.dot(ds, qb, preferred_element_type=jnp.float32)
            dqa[...] += lax.dot_general(ds, kt, (((0,), (0,)), ((), ())), preferred_element_type=jnp.float32)
            return inner

        lax.fori_loop(0, info[base + 2 * nq + b], one_tile, 0)
        for h in range(heads):
            dq_ref[m, pl.ds(row, BLK), h * HEAD : (h + 1) * HEAD] = (
                dqa[h * BLK : (h + 1) * BLK, :] * scale
            ).astype(dq_ref.dtype)
        return carry

    lax.fori_loop(0, nq, one_block, 0)

    def unsort(s, carry):
        source = info[s]
        chunk = source // 2
        row = pl.multiple_of((source % 2) * BLK, BLK)
        at = pl.multiple_of(s * BLK, BLK)
        dkv_ref[chunk, 0, pl.ds(row, BLK), :] = (dk[pl.ds(at, BLK), :] * scale).astype(dkv_ref.dtype)
        dkv_ref[chunk, 1, pl.ds(row, BLK), :] = dv[pl.ds(at, BLK), :].astype(dkv_ref.dtype)
        return carry

    lax.fori_loop(0, nk, unsort, 0)


def local_attention(info, q_all, do_all, stats, kv_all):
    chunks, _, rows, _ = kv_all.shape
    columns = chunks * rows
    members, _, width = q_all.shape
    vmem = pl.BlockSpec(memory_space=pltpu.VMEM)
    return pl.pallas_call(
        attention_kernel,
        out_shape=(
            jax.ShapeDtypeStruct((members, rows, width), jnp.bfloat16),
            jax.ShapeDtypeStruct((chunks, 2, rows, HEAD), jnp.bfloat16),
        ),
        in_specs=[pl.BlockSpec(memory_space=pltpu.SMEM), vmem, vmem, vmem, vmem],
        out_specs=(vmem, vmem),
        scratch_shapes=[
            pltpu.VMEM((columns, HEAD), jnp.bfloat16),
            pltpu.VMEM((columns, HEAD), jnp.bfloat16),
            pltpu.VMEM((columns, HEAD), jnp.float32),
            pltpu.VMEM((columns, HEAD), jnp.float32),
            pltpu.VMEM((width // HEAD * BLK, HEAD), jnp.float32),
        ],
        compiler_params=pltpu.CompilerParams(vmem_limit_bytes=40 * 1024 * 1024),
        name="local_attention",
    )(info, q_all, do_all, stats, kv_all)


def by_block(rows_of):
    heads, rows = rows_of.shape
    return rows_of.reshape(heads, 2, BLK).transpose(1, 0, 2).reshape(2, heads // 2, HEAD)


def shards(queries, keys, values, attn_out, out_grad, logsumexp, position_ids, block_map, span_blocks):
    rows, width = queries.shape
    heads = width // HEAD
    shards_of = lax.axis_size("ctx")
    me = lax.axis_index("ctx")
    z, j = me // QUAD, me % QUAD
    quads = [[c * QUAD + i for i in range(QUAD)] for c in range(shards_of // QUAD)]
    lines = [[c * QUAD + i for c in range(shards_of // QUAD)] for i in range(QUAD)]
    info = plan(block_map, span_blocks, z, j)
    cosine, sine = rope_tables(position_ids)
    grad = lax.all_to_all(out_grad, "tp", split_axis=1, concat_axis=0, tiled=True)
    q_rot = rotate(queries, cosine, sine).astype(jnp.bfloat16)
    k_rot = rotate(keys, cosine, sine).astype(jnp.bfloat16)
    delta = jnp.sum(
        (grad.astype(jnp.float32) * attn_out.astype(jnp.float32)).reshape(rows, heads, HEAD), axis=-1
    ).T
    stats = jnp.stack([by_block(logsumexp * LOG2E), by_block(delta)])
    kv = jnp.stack([k_rot, values])
    qd_all = lax.all_gather(jnp.stack([q_rot, grad]), "ctx", axis_index_groups=quads)
    stats_all = lax.all_gather(stats, "ctx", axis_index_groups=quads)
    kv_all = lax.all_gather(kv, "ctx", axis_index_groups=lines)
    dq, dkv = local_attention(info, qd_all[:, 0], qd_all[:, 1], stats_all, kv_all)
    dq = lax.psum_scatter(dq.astype(jnp.float32), "ctx", axis_index_groups=quads)
    dkv = lax.psum_scatter(dkv.astype(jnp.float32), "ctx", axis_index_groups=lines)
    grad_q = rotate(dq, cosine, -sine).astype(jnp.bfloat16)
    key_gradient = rotate(dkv[0], cosine, -sine).astype(jnp.bfloat16)
    return grad_q, key_gradient, dkv[1].astype(jnp.bfloat16)


def solution(mesh):
    return jax.shard_map(
        shards,
        mesh=mesh,
        in_specs=(
            P("ctx", "tp"),
            P("ctx", "tp"),
            P("ctx", "tp"),
            P("ctx", "tp"),
            P(("ctx", "tp"), None),
            P("tp", "ctx"),
            P(None, "ctx"),
            P(),
            P(),
        ),
        out_specs=(P("ctx", "tp"), P("ctx", "tp"), P("ctx", "tp")),
        check_vma=False,
    )
```

time: 870 us -> 301 us (0.35)
  the two profiles are of different devices: /device:TPU:134 before, /device:TPU:2 now
where the time goes in v1:
time: 301 us
  waiting for transfers between devices  223 us (74%)
  Pallas kernels  25.5 us (8%)
  between operations  14 us (5%)
  local copies, waits for them, and re-layouts  11.2 us (4%)
  other arithmetic  11.2 us (4%)
  starting transfers between devices  9.36 us (3%)
  blocking collectives  6.69 us (2%)
    reduce_scatter x1, waiting for transfers between devices, shards(): lax.psum_scatter(dkv.astype(jnp.float32), 'ctx', axis_index_groups=lines)  74.4 us
    all_gather x1, waiting for transfers between devices, shards(): kv_all = lax.all_gather(kv, 'ctx', axis_index_groups=lines)  71.4 us
    reduce_scatter x1, waiting for transfers between devices, shards(): lax.psum_scatter(dq.astype(jnp.float32), 'ctx', axis_index_groups=quads)  51.1 us
    pallas_call x1, Pallas kernels, local_attention(): pl.pallas_call(attention_kernel, out_shape=(jax.ShapeDtypeStruct((members...  25.5 us
    all_gather x1, waiting for transfers between devices, shards(): lax.all_gather(jnp.stack([q_rot, grad]), 'ctx', axis_index_groups=quads)  25.4 us
    all_to_all x1, starting transfers between devices, shards(): lax.all_to_all(out_grad, 'tp', split_axis=1, concat_axis=0, tiled=True)  9.23 us
    all_gather x1, blocking collectives, shards(): stats_all = lax.all_gather(stats, 'ctx', axis_index_groups=quads)  6.69 us
  transfers between devices with their start and end apart: 5, of which 5 were waited for; matrix products, arithmetic and copies ran while one was open for 4% of the time, Pallas kernels for 0%

profile of v1, /device:TPU:2, one launch (start us, length us, event | category | flops | bytes accessed | tf_op | source)
XLA Modules:
  0.0 300.8 jit_solution(9986550906694835530)
XLA Ops:
  7.2 1.7 copy.55
  8.8 9.2 %all-to-all-start = ((bf16[16,8,1024]{2,0,1:T(8,128)(2,1)}), bf16[16,8,1024]{2,0,1:T(8,128)(2,1)S(1)}, u32[]{:S(2)}, u32[]{:S(2)}) async-start(bf16[16,8,1024]{2,0,1:T(8,128)(2,1)} %bitcast.89), calls=%async_computation | async-start | bytes 524288 | tf_op jit(solution)/shard_map/all_to_all | solution.py:175
  18.1 0.0 all-gather.6.cloned.1.call-start
  18.1 0.8 slice_bitcast_fusion.9
  18.9 0.8 convert_bitcast_fusion.1
  19.7 0.1 slice_bitcast_fusion.5
  19.7 1.0 convert_bitcast_fusion
  20.7 0.1 copy.40
  20.8 0.0 copy-start.4
  20.9 0.2 fusion.14
  21.1 0.4 fusion.11
  21.4 0.2 maximum_multiply_fusion
  21.6 0.0 copy-start.7
  21.7 0.0 copy-start.8
  21.7 0.0 copy-start.9
  21.7 0.0 copy-start.10
  21.7 0.0 copy-start.5
  21.8 0.8 copy-done.1
  22.5 0.2 fusion.4
  22.8 0.5 all-to-all-done
  23.3 0.9 pad_maximum_fusion
  24.2 0.0 all-gather.6.cloned.1.call-update
  24.2 0.0 all-gather.8.cloned.1.call-start
  24.3 0.6 pad_maximum_fusion.1
  24.9 0.0 all-gather.8.cloned.1.call-update
  24.9 0.0 reduce-scatter.3.cloned.1.call-start
  25.0 0.1 reshape.399
  25.1 0.1 stack_reshape.6
  25.2 0.0 copy-done.9
  25.2 0.2 reshape.397
  25.4 0.1 lt.83
  25.5 0.1 broadcast_multiply_fusion.1
  25.6 0.2 convert_reduce_fusion
  25.8 0.1 select_reduce_fusion
  25.9 0.2 select_reduce_fusion.2
  26.1 0.2 convert_reduce_fusion.1
  26.3 0.1 concatenate.29.info
  26.4 0.1 fusion.3
  26.5 0.1 copy.42
  26.6 0.2 reduce_sum.59
  26.8 0.1 copy.35
  26.9 0.1 stack_reshape.7
  26.9 6.7 %all-gather.1 = f32[8,2,4,128]{3,2,1,0:T(4,128)S(1)} all-gather(f32[2,2,4,128]{3,2,1,0:T(4,128)S(1)} %pad_maximum_fusion.2), channel_id=3, replica_groups={{0,8,16,24},{32,40,48,56},{64,72,80,88},{96,104,112,120},{128,136,144,1..., dimensions={0}, use_global_device_ids=true | all-gather | bytes 40960 | tf_op jit(solution)/shard_map/all_gather | solution.py:184
  33.6 25.4 %all-gather.6.cloned.1.call-done = bf16[8,128,1024]{2,1,0:T(8,128)(2,1)} async-done(((bf16[2,128,1024]{2,1,0:T(8,128)(2,1)}), bf16[8,128,1024]{2,1,0:T(8,128)(2,1)}) %all-gather.6.cloned.1.call-update) | async-done | bytes 2097168 | tf_op jit(solution)/shard_map/all_gather | solution.py:183
  59.0 1.8 slice_bitcast_fusion
  60.8 71.4 %all-gather.8.cloned.1.call-done = bf16[32,128,128]{2,1,0:T(8,128)(2,1)} async-done(((bf16[2,128,128]{2,1,0:T(8,128)(2,1)}), bf16[32,128,128]{2,1,0:T(8,128)(2,1)}) %all-gather.8.cloned.1.call-update) | async-done | bytes 1048592 | tf_op jit(solution)/shard_map/all_gather | solution.py:185
  132.2 1.2 copy-done
  133.5 25.5 %local_attention.1 = (bf16[4,128,1024]{2,1,0:T(8,128)(2,1)S(1)}, bf16[16,2,128,128]{3,2,1,0:T(8,128)(2,1)S(1)}) custom-call(s32[88]{0:T(128)S(1)} %concatenate.29.info, bf16[4,128,1024]{2,1,0:T(8,128)(2,1)S(1)} %get-tuple-element.12.q_ref, bf16[4,128,1024]{2,1,0:T(8,128)(2,1)S(1)} %get-tuple-element.11.do_ref, f32[4,2,2,4,128]{4,3,2,1,0:T(4,128)S(1)} %bitcast.92, ...), custom_call_target="tpu_custom_call" | custom-call | tf_op jit(solution)/shard_map/local_attention/pallas_call | solution.py:140
  159.0 1.6 convert_element_type.81
  160.5 0.0 reduce-scatter.3.cloned.1.call-update
  160.6 0.0 reduce-scatter.5.cloned.1.call-start
  160.6 1.5 convert_element_type.83
  162.2 0.0 reduce-scatter.5.cloned.1.call-update
  162.2 51.1 %reduce-scatter.3.cloned.1.call-done = f32[1,128,1024]{2,1,0:T(8,128)} async-done(((f32[4,128,1024]{2,1,0:T(8,128)}), f32[1,128,1024]{2,1,0:T(8,128)}) %reduce-scatter.3.cloned.1.call-update) | async-done | bytes 524304 | tf_op jit(solution)/shard_map/reduce_scatter | solution.py:187
  213.3 1.1 copy.43
  214.4 0.2 fusion.13
  214.6 74.4 %reduce-scatter.5.cloned.1.call-done = f32[1,2,128,128]{3,2,1,0:T(8,128)} async-done(((f32[16,2,128,128]{3,2,1,0:T(8,128)}), f32[1,2,128,128]{3,2,1,0:T(8,128)}) %reduce-scatter.5.cloned.1.call-update) | async-done | bytes 131088 | tf_op jit(solution)/shard_map/reduce_scatter | solution.py:188
  289.0 0.8 slice_bitcast_fusion.6
  289.8 0.1 slice_bitcast_fusion.3
  289.9 1.8 fusion.8
  291.7 0.2 maximum_multiply_fusion.1
  291.9 1.5 fusion.10
  293.4 0.0 copy-done.3
  293.4 0.9 fusion.2
  (23 shorter events, 0.2 us)
Async XLA Ops:
  8.8 14.5 %all-to-all-start = ((bf16[16,8,1024]{2,0,1:T(8,128)(2,1)}), bf16[16,8,1024]{2,0,1:T(8,128)(2,1)S(1)}, u32[]{:S(2)}, u32[]{:S(2)}) async-start(bf16[16,8,1024]{2,0,1:T(8,128)(2,1)} %bitcast.89), calls=%async_computation | async-start | bytes 524288 | tf_op jit(solution)/shard_map/all_to_all | solution.py:175
  18.1 41.0 %all-gather.6.cloned.1.call-start = ((), (), s32[]{:S(2)}) async-start(), calls=%async_computation.5 | async-start | bytes 2621440 | tf_op jit(solution)/shard_map/all_gather | solution.py:183
  19.7 1.4 copy-start.6
  20.8 1.7 copy-start.4
  21.6 2.6 copy-start.7
  21.7 3.3 %copy-start.8 = (f32[8,128]{1,0:T(8,128)S(1)}, f32[8,128]{1,0:T(8,128)}, u32[]{:S(2)}) copy-start(f32[8,128]{1,0:T(8,128)} %param.14) | copy-start | bytes 12292
  21.7 3.5 %copy-start.9 = (s32[128]{0:T(128)S(1)}, s32[128]{0:T(128)}, u32[]{:S(2)}) copy-start(s32[128]{0:T(128)} %param.16) | copy-start | bytes 1540
  21.7 4.2 %copy-start.10 = (s32[16,2]{0,1:T(2,128)S(1)}, s32[16,2]{0,1:T(2,128)}, u32[]{:S(2)}) copy-start(s32[16,2]{0,1:T(2,128)} %param.17) | copy-start | bytes 388
  21.7 4.7 %copy-start.5 = (bf16[128,1024]{1,0:T(8,128)(2,1)S(1)}, bf16[128,1024]{1,0:T(8,128)(2,1)}, u32[]{:S(2)}) copy-start(bf16[128,1024]{1,0:T(8,128)(2,1)} %param.12) | copy-start | bytes 786436
  21.7 0.8 copy-start.1
  24.2 108.0 %all-gather.8.cloned.1.call-start = ((), (), s32[]{:S(2)}) async-start(), calls=%async_computation.6 | async-start | bytes 1114112 | tf_op jit(solution)/shard_map/all_gather | solution.py:185
  24.9 188.3 %reduce-scatter.3.cloned.1.call-start = ((), (), s32[]{:S(2)}) async-start(), calls=%async_computation.3 | async-start | bytes 2621440 | tf_op jit(solution)/shard_map/reduce_scatter | solution.py:187
  132.2 1.2 copy-start
  160.6 128.4 %reduce-scatter.5.cloned.1.call-start = ((), (), s32[]{:S(2)}) async-start(), calls=%async_computation.4 | async-start | bytes 2228224 | tf_op jit(solution)/shard_map/reduce_scatter | solution.py:188
  214.4 79.0 %copy-start.2 = (f32[128,8,128]{2,1,0:T(8,128)S(1)}, f32[128,8,128]{2,1,0:T(8,128)}, u32[]{:S(2)}) copy-start(f32[128,8,128]{2,1,0:T(8,128)} %copy-done.1) | copy-start | bytes 1572868
  214.4 79.0 %copy-start.3 = (f32[1,128,1024]{2,1,0:T(8,128)S(1)}, f32[1,128,1024]{2,1,0:T(8,128)}, u32[]{:S(2)}) copy-start(f32[1,128,1024]{2,1,0:T(8,128)} %reduce-scatter.3.cloned.1.call-done) | copy-start | bytes 1572868
Sparse Core Ops, SparseCore 0:
  24.3 34.6 all-gather.5
  61.7 70.4 all-gather.7
  160.7 52.5 reduce-scatter.2
  216.2 72.7 reduce-scatter.4

commit v2 on v1

--- a/solution.py
+++ b/solution.py
@@ -1,3 +1,4 @@
+import functools
 import math
 
 import jax
@@ -29,13 +30,6 @@
     angles = picked.astype(jnp.float32) * inverse[None, :]
     sign = jnp.where(jnp.arange(HEAD) < half, -1.0, 1.0).astype(jnp.float32)
     return jnp.cos(angles), jnp.sin(angles) * sign[None, :]
-
-
-def rotate(field, cosine, sine):
-    rows, width = field.shape
-    x = field.astype(jnp.float32).reshape(rows, width // HEAD, HEAD)
-    out = x * cosine[:, None, :] + jnp.roll(x, HEAD // 2, axis=-1) * sine[:, None, :]
-    return out.reshape(rows, width)
 
 
 def plan(block_map, span_blocks, z, j):
@@ -157,38 +151,323 @@
     )(info, q_all, do_all, stats, kv_all)
 
 
-def by_block(rows_of):
-    heads, rows = rows_of.shape
-    return rows_of.reshape(heads, 2, BLK).transpose(1, 0, 2).reshape(2, heads // 2, HEAD)
-
-
-def shards(queries, keys, values, attn_out, out_grad, logsumexp, position_ids, block_map, span_blocks):
+MESH = pl.DeviceIdType.MESH
+
+
+def places(heads_axis):
+    me = lax.axis_index("ctx")
+    z, j = me // QUAD, me % QUAD
+    yh, core = j // 2, j % 2
+    return me, z, j, yh, core, lax.axis_index(heads_axis)
+
+
+def signal_all(barrier, peers):
+    for peer in peers:
+        pl.semaphore_signal(barrier, inc=1, device_id=peer, device_id_type=MESH)
+    pl.semaphore_wait(barrier, len(peers))
+
+
+def send(source, target, send_sem, recv_sem, peer):
+    return pltpu.make_async_remote_copy(
+        src_ref=source,
+        dst_ref=target,
+        send_sem=send_sem,
+        recv_sem=recv_sem,
+        device_id=peer,
+        device_id_type=MESH,
+    )
+
+
+def gather_kernel(
+    nz, ntp, q_in, k_in, v_in, out_in, grad_in, lse_in, cos_in, sin_in,
+    q_all, do_all, stats, kv_all,
+    do_send, do_recv, own_sem, ring_send, ring_recv, q_send, q_recv, fwd_send, fwd_recv, st_send, st_recv,
+):
+    me, z, j, yh, core, tp = places("tp")
+    rows, width = q_in.shape
+    heads = width // HEAD
+    slab = rows // ntp
+    n = nz * QUAD
+    right = {"ctx": (me + QUAD) % n, "tp": tp}
+    left = {"ctx": (me + n - QUAD) % n, "tp": tp}
+    to_core = me + 1 - 2 * core
+    to_y = me + 2 - 4 * yh
+    diagonal = to_core + 2 - 4 * yh
+    core_peer = {"ctx": to_core, "tp": tp}
+    y_peer = {"ctx": to_y, "tp": tp}
+    far_peer = {"ctx": diagonal, "tp": tp}
+    j_y = j + 2 - 4 * yh
+    others = [{"ctx": where, "tp": (tp + i) % ntp} for where in (me, to_y) for i in range(1, ntp)]
+    signal_all(pltpu.get_barrier_semaphore(), [right, left, core_peer, y_peer, far_peer, *others])
+
+    mine = pl.ds(pl.multiple_of(tp * slab, slab), slab)
+    copies = []
+    own = None
+    for i in range(ntp):
+        t = (tp + i) % ntp
+        part = grad_in.at[:, pl.ds(pl.multiple_of(t * width, width), width)]
+        for a, where in enumerate((me, to_y)):
+            if i == 0 and a == 0:
+                own = pltpu.make_async_copy(part, do_all.at[j, mine, :], own_sem)
+                own.start()
+            else:
+                copies.append(
+                    send(part, do_all.at[j, mine, :], do_send.at[a, i], do_recv.at[a, i], {"ctx": where, "tp": t})
+                )
+                copies[-1].start()
+
+    cosine, sine = cos_in[...], sin_in[...]
+    k = k_in[...].astype(jnp.float32)
+    kv_all[z, 0] = (k * cosine + pltpu.roll(k, HEAD // 2, 1) * sine).astype(jnp.bfloat16)
+    kv_all[z, 1] = v_in[...]
+    hops = (nz // 2, nz // 2 - 1)
+
+    def hop(d, s, piece):
+        slot = (z - s + nz) % nz if d == 0 else (z + s) % nz
+        ref = kv_all.at[slot, piece]
+        return send(ref, ref, ring_send.at[d, s, piece], ring_recv.at[d, s, piece], right if d == 0 else left)
+
+    def arrived(d, s, piece):
+        slot = (z - s - 1 + nz) % nz if d == 0 else (z + s + 1) % nz
+        ref = kv_all.at[slot, piece]
+        return send(ref, ref, ring_send.at[d, s, piece], ring_recv.at[d, s, piece], right if d == 0 else left)
+
+    for piece in range(2):
+        for d in range(2):
+            if hops[d] > 0:
+                hop(d, 0, piece).start()
+
+    for h in range(heads):
+        at = slice(h * HEAD, (h + 1) * HEAD)
+        x = q_in[:, at].astype(jnp.float32)
+        q_all[j, :, at] = (x * cosine + pltpu.roll(x, HEAD // 2, 1) * sine).astype(jnp.bfloat16)
+    q_y = send(q_all.at[j], q_all.at[j], q_send.at[0], q_recv.at[0], y_peer)
+    q_core = send(q_all.at[j], q_all.at[j], q_send.at[1], q_recv.at[1], core_peer)
+    q_y.start()
+    q_core.start()
+
+    def steps(first, last):
+        def one(s, carry):
+            for piece in range(2):
+                for d in range(2):
+                    arrived(d, s - 1, piece).wait_recv()
+                    hop(d, s, piece).start()
+            return carry
+
+        lax.fori_loop(first, last, one, 0)
+
+    middle = (1 + hops[1]) // 2
+    steps(1, middle)
+
+    own.wait()
+    for i in range(1, ntp):
+        t = (tp - i + ntp) % ntp
+        there = do_all.at[j, pl.ds(pl.multiple_of(t * slab, slab), slab), :]
+        send(there, there, do_send.at[0, i], do_recv.at[0, i], core_peer).wait_recv()
+    forward = [send(do_all.at[j], do_all.at[j], fwd_send.at[0], fwd_recv.at[0], core_peer)]
+    forward[0].start()
+    lane = lax.broadcasted_iota(jnp.int32, (1, HEAD), 1)
+    for k2 in range(heads // 2):
+        pair = []
+        for h in (2 * k2, 2 * k2 + 1):
+            at = slice(h * HEAD, (h + 1) * HEAD)
+            product = do_all[j, :, at].astype(jnp.float32) * out_in[:, at].astype(jnp.float32)
+            pair.append((lse_in[h : h + 1, :] * LOG2E, jnp.sum(product.T, axis=0, keepdims=True)))
+        for what in range(2):
+            a, b = pair[0][what], pair[1][what]
+            stats[j, what, 0, k2 : k2 + 1, :] = jnp.where(lane < BLK, a, pltpu.roll(b, BLK, 1))
+            stats[j, what, 1, k2 : k2 + 1, :] = jnp.where(lane < BLK, pltpu.roll(a, BLK, 1), b)
+    small = [
+        send(stats.at[j], stats.at[j], st_send.at[i], st_recv.at[i], peer)
+        for i, peer in enumerate((core_peer, y_peer, far_peer))
+    ]
+    for copy in small:
+        copy.start()
+
+    send(q_all.at[j_y], q_all.at[j_y], q_send.at[0], q_recv.at[0], y_peer).wait_recv()
+    forward.append(send(q_all.at[j_y], q_all.at[j_y], fwd_send.at[1], fwd_recv.at[1], core_peer))
+    forward[1].start()
+    steps(middle, hops[1])
+    for i in range(ntp):
+        t = (tp - i + ntp) % ntp
+        there = do_all.at[j_y, pl.ds(pl.multiple_of(t * slab, slab), slab), :]
+        send(there, there, do_send.at[1, i], do_recv.at[1, i], core_peer).wait_recv()
+    forward.append(send(do_all.at[j_y], do_all.at[j_y], fwd_send.at[2], fwd_recv.at[2], core_peer))
+    forward[2].start()
+
+    for piece in range(2):
+        if hops[1] > 0:
+            arrived(0, hops[1] - 1, piece).wait_recv()
+            hop(0, hops[1], piece).start()
+            arrived(1, hops[1] - 1, piece).wait_recv()
+    for piece in range(2):
+        arrived(0, hops[0] - 1, piece).wait_recv()
+    for d in range(2):
+        for s in range(hops[d]):
+            for piece in range(2):
+                hop(d, s, piece).wait_send()
+    for copy in copies:
+        copy.wait_send()
+    q_y.wait_send()
+    q_core.wait()
+    for copy in forward:
+        copy.wait()
+    for copy in small:
+        copy.wait()
+
+
+def gather(queries, keys, values, attn_out, out_grad, logsumexp, cosine, sine):
     rows, width = queries.shape
     heads = width // HEAD
-    shards_of = lax.axis_size("ctx")
+    nz = lax.axis_size("ctx") // QUAD
+    ntp = lax.axis_size("tp")
+    vmem = pl.BlockSpec(memory_space=pltpu.VMEM)
+    dma = pltpu.SemaphoreType.DMA
+    return pl.pallas_call(
+        functools.partial(gather_kernel, nz, ntp),
+        out_shape=(
+            jax.ShapeDtypeStruct((QUAD, rows, width), jnp.bfloat16),
+            jax.ShapeDtypeStruct((QUAD, rows, width), jnp.bfloat16),
+            jax.ShapeDtypeStruct((QUAD, 2, 2, heads // 2, HEAD), jnp.float32),
+            jax.ShapeDtypeStruct((nz, 2, rows, HEAD), jnp.bfloat16),
+        ),
+        in_specs=[vmem, vmem, vmem, vmem, pl.BlockSpec(memory_space=pl.ANY), vmem, vmem, vmem],
+        out_specs=(vmem, vmem, vmem, vmem),
+        scratch_shapes=[
+            dma((2, ntp)), dma((2, ntp)), dma, dma((2, nz // 2, 2)), dma((2, nz // 2, 2)),
+            dma((2,)), dma((2,)), dma((3,)), dma((3,)), dma((3,)), dma((3,)),
+        ],
+        compiler_params=pltpu.CompilerParams(
+            vmem_limit_bytes=40 * 1024 * 1024, collective_id=0, has_side_effects=True
+        ),
+        name="gather_inputs",
+    )(queries, keys, values, attn_out, out_grad, logsumexp, cosine, sine)
+
+
+def reduce_kernel(
+    nz, dq_in, dkv_in, cos_in, sin_in, gq_out, gk_out, gv_out,
+    ring, first, second, total, ring_send, ring_recv, core_send, core_recv, y_send, y_recv,
+):
+    me, z, j, yh, core, tp = places("tp")
+    rows, width = gq_out.shape
+    heads = width // HEAD
+    n = nz * QUAD
+    right = {"ctx": (me + QUAD) % n, "tp": tp}
+    left = {"ctx": (me + n - QUAD) % n, "tp": tp}
+    core_peer = {"ctx": me + 1 - 2 * core, "tp": tp}
+    y_peer = {"ctx": me + 2 - 4 * yh, "tp": tp}
+    signal_all(pltpu.get_barrier_semaphore(), [right, left, core_peer, y_peer])
+    hops = (nz // 2, nz // 2 - 1)
+
+    def owner(d, s):
+        return (z + hops[0] - s) % nz if d == 0 else (z - hops[1] + s + nz) % nz
+
+    def hop(d, s, piece, source):
+        return send(
+            source, ring.at[d, s, piece], ring_send.at[d, s, piece], ring_recv.at[d, s, piece],
+            right if d == 0 else left,
+        )
+
+    for piece in range(2):
+        for d in range(2):
+            if hops[d] > 0:
+                hop(d, 0, piece, dkv_in.at[owner(d, 0), piece]).start()
+    wanted = [2 * (1 - yh) + core, j]
+    to_core = [
+        send(dq_in.at[m + 1 - 2 * core], first.at[i], core_send.at[i], core_recv.at[i], core_peer)
+        for i, m in enumerate(wanted)
+    ]
+    for copy in to_core:
+        copy.start()
+    to_core[0].wait_recv()
+    total[...] = (dq_in[wanted[0]].astype(jnp.float32) + first[0].astype(jnp.float32)).astype(jnp.bfloat16)
+    to_y = send(total, second, y_send, y_recv, y_peer)
+    to_y.start()
+
+    def step(d, s, piece):
+        hop(d, s - 1, piece, ring.at[d, s - 1, piece]).wait_recv()
+        ring[d, s - 1, piece] = (
+            ring[d, s - 1, piece].astype(jnp.float32) + dkv_in[owner(d, s), piece].astype(jnp.float32)
+        ).astype(jnp.bfloat16)
+        hop(d, s, piece, ring.at[d, s - 1, piece]).start()
+
+    def steps(s, carry):
+        for piece in range(2):
+            for d in range(2):
+                step(d, s, piece)
+        return carry
+
+    lax.fori_loop(1, hops[1], steps, 0)
+    if hops[1] > 0:
+        for piece in range(2):
+            step(0, hops[1], piece)
+    to_core[1].wait_recv()
+    to_y.wait_recv()
+    cosine, sine = cos_in[...], sin_in[...]
+    for h in range(heads):
+        at = slice(h * HEAD, (h + 1) * HEAD)
+        x = (
+            dq_in[j, :, at].astype(jnp.float32)
+            + first[1, :, at].astype(jnp.float32)
+            + second[:, at].astype(jnp.float32)
+        )
+        gq_out[:, at] = (x * cosine - pltpu.roll(x, HEAD // 2, 1) * sine).astype(jnp.bfloat16)
+    for piece in range(2):
+        x = dkv_in[z, piece].astype(jnp.float32)
+        for d in range(2):
+            if hops[d] > 0:
+                last = ring.at[d, hops[d] - 1, piece]
+                hop(d, hops[d] - 1, piece, last).wait_recv()
+                x = x + last[...].astype(jnp.float32)
+        if piece == 0:
+            gk_out[...] = (x * cosine - pltpu.roll(x, HEAD // 2, 1) * sine).astype(jnp.bfloat16)
+        else:
+            gv_out[...] = x.astype(jnp.bfloat16)
+    for d in range(2):
+        for s in range(hops[d]):
+            for piece in range(2):
+                hop(d, s, piece, ring.at[d, s, piece]).wait_send()
+    for copy in (*to_core, to_y):
+        copy.wait_send()
+
+
+def scatter(dq, dkv, cosine, sine):
+    nz, _, rows, _ = dkv.shape
+    width = dq.shape[2]
+    vmem = pl.BlockSpec(memory_space=pltpu.VMEM)
+    dma = pltpu.SemaphoreType.DMA
+    return pl.pallas_call(
+        functools.partial(reduce_kernel, nz),
+        out_shape=(
+            jax.ShapeDtypeStruct((rows, width), jnp.bfloat16),
+            jax.ShapeDtypeStruct((rows, HEAD), jnp.bfloat16),
+            jax.ShapeDtypeStruct((rows, HEAD), jnp.bfloat16),
+        ),
+        in_specs=[vmem] * 4,
+        out_specs=(vmem, vmem, vmem),
+        scratch_shapes=[
+            pltpu.VMEM((2, nz // 2, 2, rows, HEAD), jnp.bfloat16),
+            pltpu.VMEM((2, rows, width), jnp.bfloat16),
+            pltpu.VMEM((rows, width), jnp.bfloat16),
+            pltpu.VMEM((rows, width), jnp.bfloat16),
+            dma((2, nz // 2, 2)), dma((2, nz // 2, 2)), dma((2,)), dma((2,)), dma, dma,
+        ],
+        compiler_params=pltpu.CompilerParams(
+            vmem_limit_bytes=40 * 1024 * 1024, collective_id=1, has_side_effects=True
+        ),
+        name="scatter_gradients",
+    )(dq, dkv, cosine, sine)
+
+
+def shards(queries, keys, values, attn_out, out_grad, logsumexp, position_ids, block_map, span_blocks):
     me = lax.axis_index("ctx")
-    z, j = me // QUAD, me % QUAD
-    quads = [[c * QUAD + i for i in range(QUAD)] for c in range(shards_of // QUAD)]
-    lines = [[c * QUAD + i for c in range(shards_of // QUAD)] for i in range(QUAD)]
-    info = plan(block_map, span_blocks, z, j)
+    info = plan(block_map, span_blocks, me // QUAD, me % QUAD)
     cosine, sine = rope_tables(position_ids)
-    grad = lax.all_to_all(out_grad, "tp", split_axis=1, concat_axis=0, tiled=True)
-    q_rot = rotate(queries, cosine, sine).astype(jnp.bfloat16)
-    k_rot = rotate(keys, cosine, sine).astype(jnp.bfloat16)
-    delta = jnp.sum(
-        (grad.astype(jnp.float32) * attn_out.astype(jnp.float32)).reshape(rows, heads, HEAD), axis=-1
-    ).T
-    stats = jnp.stack([by_block(logsumexp * LOG2E), by_block(delta)])
-    kv = jnp.stack([k_rot, values])
-    qd_all = lax.all_gather(jnp.stack([q_rot, grad]), "ctx", axis_index_groups=quads)
-    stats_all = lax.all_gather(stats, "ctx", axis_index_groups=quads)
-    kv_all = lax.all_gather(kv, "ctx", axis_index_groups=lines)
-    dq, dkv = local_attention(info, qd_all[:, 0], qd_all[:, 1], stats_all, kv_all)
-    dq = lax.psum_scatter(dq.astype(jnp.float32), "ctx", axis_index_groups=quads)
-    dkv = lax.psum_scatter(dkv.astype(jnp.float32), "ctx", axis_index_groups=lines)
-    grad_q = rotate(dq, cosine, -sine).astype(jnp.bfloat16)
-    key_gradient = rotate(dkv[0], cosine, -sine).astype(jnp.bfloat16)
-    return grad_q, key_gradient, dkv[1].astype(jnp.bfloat16)
+    q_all, do_all, stats, kv_all = gather(
+        queries, keys, values, attn_out, out_grad, logsumexp, cosine, sine
+    )
+    dq, dkv = local_attention(info, q_all, do_all, stats, kv_all)
+    return scatter(dq, dkv, cosine, sine)
 
 
 def solution(mesh):

time: 301 us -> 111 us (0.37)
  the two profiles are of different devices: /device:TPU:2 before, /device:TPU:8 now
where the time goes in v2:
time: 111 us; the launch traced here: 110 us
  Pallas kernels  100 us (90%)
  local copies, waits for them, and re-layouts  7.55 us (7%)
  other arithmetic  1.82 us (2%)
    pallas_call x1, Pallas kernels, gather(): pl.pallas_call(functools.partial(gather_kernel, nz, ntp), out_shape=(jax....  41.9 us
    pallas_call x1, Pallas kernels, scatter(): pl.pallas_call(functools.partial(reduce_kernel, nz), out_shape=(jax.Shape...  34.6 us
    pallas_call x1, Pallas kernels, local_attention(): pl.pallas_call(attention_kernel, out_shape=(jax.ShapeDtypeStruct((members...  23.7 us
    unnamed x15, local copies, waits for them, and re-layouts  4.99 us

profile of v2, /device:TPU:8, one launch (start us, length us, event | category | flops | bytes accessed | tf_op | source)
XLA Modules:
  0.0 110.3 jit_solution(3031105531883130142)
XLA Ops:
  0.6 0.0 copy-start
  0.7 0.8 broadcast_multiply_fusion
  1.4 0.8 slice_bitcast_fusion.4
  2.2 0.2 select_reduce_fusion.2
  2.4 0.8 slice_bitcast_fusion.2
  3.2 0.8 reshape.46
  4.1 0.1 lt.83
  4.2 0.2 convert_reduce_fusion.1
  4.3 0.2 convert_reduce_fusion
  4.5 0.1 select_reduce_fusion
  4.7 0.1 concatenate.3.info
  4.7 0.0 copy-start.3
  4.7 0.0 copy-start.5
  4.7 0.4 sine_multiply_fusion
  5.1 0.0 copy-done
  5.1 0.4 copy-done.3
  5.5 0.0 copy-done.5
  5.5 0.0 copy-start.1
  5.5 0.9 copy-done.1
  6.5 0.0 copy-start.2
  6.5 0.9 copy-done.2
  7.4 0.0 copy-start.4
  7.4 0.8 copy-done.4
  8.2 41.9 %gather_inputs.1 = (bf16[4,128,1024]{2,1,0:T(8,128)(2,1)S(1)}, bf16[4,128,1024]{2,1,0:T(8,128)(2,1)S(1)}, f32[4,2,2,4,128]{4,3,2,1,0:T(4,128)S(1)}, bf16[16,2,128,128]{3,2,1,0:T(8,128)(2,1)S(1)}) custom-call(bf16[128,1024]{1,0:T(8,128)(2,1)S(1)} %copy-done, bf16[128,128]{1,0:T(8,128)(2,1)S(1)} %copy-done.3, bf16[128,128]{1,0:T(8,128)(2,1)S(1)} %copy-done.4, ...), custom_call_target="tpu_custom_call" | custom-call | tf_op jit(solution)/shard_map/gather_inputs/pallas_call | solution.py:326
  50.1 23.7 %local_attention.1 = (bf16[4,128,1024]{2,1,0:T(8,128)(2,1)S(1)}, bf16[16,2,128,128]{3,2,1,0:T(8,128)(2,1)S(1)}) custom-call(s32[88]{0:T(128)S(1)} %concatenate.3.info, bf16[4,128,1024]{2,1,0:T(8,128)(2,1)S(1)} %get-tuple-element.9.q_ref, bf16[4,128,1024]{2,1,0:T(8,128)(2,1)S(1)} %get-tuple-element.10.do_ref, ...), custom_call_target="tpu_custom_call" | custom-call | tf_op jit(solution)/shard_map/local_attention/pallas_call | solution.py:134
  73.8 34.6 %scatter_gradients.1 = (bf16[128,1024]{1,0:T(8,128)(2,1)S(1)}, bf16[128,128]{1,0:T(8,128)(2,1)S(1)}, bf16[128,128]{1,0:T(8,128)(2,1)S(1)}) custom-call(bf16[4,128,1024]{2,1,0:T(8,128)(2,1)S(1)} %get-tuple-element.13.dq_in, bf16[16,2,128,128]{3,2,1,0:T(8,128)(2,1)S(1)} %get-tuple-element.14.dkv_in, f32[128,128]{1,0:T(8,128)S(1)} %get-tuple-element.20.cos_in, ...), custom_call_target="tpu_custom_call" | custom-call | tf_op jit(solution)/shard_map/scatter_gradients/pallas_call | solution.py:439
  108.4 0.7 copy.15
  109.1 0.6 copy.16
  109.7 0.6 copy.17
  (5 shorter events, 0.1 us)
Async XLA Ops:
  0.6 4.5 %copy-start = (bf16[128,1024]{1,0:T(8,128)(2,1)S(1)}, bf16[128,1024]{1,0:T(8,128)(2,1)}, u32[]{:S(2)}) copy-start(bf16[128,1024]{1,0:T(8,128)(2,1)} %q_in.1) | copy-start | bytes 786436
  4.7 0.8 copy-start.3
  4.7 0.8 copy-start.5
  5.5 1.0 copy-start.1
  6.5 0.9 copy-start.2
  7.4 0.8 copy-start.4

commit v3 on v1

v3 whole, which is shorter than its diff:
```python
import functools
import math

import jax
import jax.numpy as jnp
from jax import lax
from jax.experimental import pallas as pl
from jax.experimental.pallas import tpu as pltpu
from jax.sharding import PartitionSpec as P

HEAD = 128
BLK = 64
QUAD = 4
THETA = 1000000.0
LOG2E = 1.4426950408889634


def rope_tables(position_ids):
    half = HEAD // 2
    pair = jnp.arange(HEAD, dtype=jnp.int32) % half
    inverse = jnp.exp(pair.astype(jnp.float32) * jnp.float32(-2.0 * math.log(THETA) / HEAD))
    first_cut = HEAD // 8
    second_cut = first_cut + 3 * HEAD // 16
    picked = jnp.where(
        pair[None, :] < first_cut,
        position_ids[0][:, None],
        jnp.where(pair[None, :] < second_cut, position_ids[1][:, None], position_ids[2][:, None]),
    )
    angles = picked.astype(jnp.float32) * inverse[None, :]
    sign = jnp.where(jnp.arange(HEAD) < half, -1.0, 1.0).astype(jnp.float32)
    return jnp.cos(angles), jnp.sin(angles) * sign[None, :]


MESH = pl.DeviceIdType.MESH


def signal_all(barrier, peers):
    for peer in peers:
        pl.semaphore_signal(barrier, inc=1, device_id=peer, device_id_type=MESH)
    pl.semaphore_wait(barrier, len(peers))


def send(source, target, send_sem, recv_sem, peer):
    return pltpu.make_async_remote_copy(
        src_ref=source,
        dst_ref=target,
        send_sem=send_sem,
        recv_sem=recv_sem,
        device_id=peer,
        device_id_type=MESH,
    )


def step_kernel(
    nz, ntp, map_in, span_in, q_in, k_in, v_in, out_in, grad_in, lse_in, cos_in, sin_in,
    gq_out, gk_out, gv_out,
    q_raw, out_raw, lse_raw, k_raw, q_all, do_all, stats, kv, part, dq, dq_go, first, second, carry, stage, back, limits,
    local, do_send, do_recv, kv_send, kv_recv, q_send, q_recv, fwd_send, fwd_recv, st_send, st_recv,
    rs_send, rs_recv, dq_send, dq_recv,
):
    me = lax.axis_index("ctx")
    tp = lax.axis_index("tp")
    z, j = me // QUAD, me % QUAD
    yh, core = j // 2, j % 2
    rows, width = gq_out.shape
    heads = width // HEAD
    slab = rows // ntp
    n = nz * QUAD
    half = nz // 2
    far = (half, half - 1)
    scale = 1.0 / math.sqrt(HEAD)
    at_core = me + 1 - 2 * core
    at_y = me + 2 - 4 * yh
    core_peer = {"ctx": at_core, "tp": tp}
    y_peer = {"ctx": at_y, "tp": tp}
    cross_peer = {"ctx": at_core + 2 - 4 * yh, "tp": tp}
    along = {k: {"ctx": (me + QUAD * k + n) % n, "tp": tp} for k in (1, 2, -1, -2)}

    loads = [
        pltpu.make_async_copy(source, target, local.at[i])
        for i, (source, target) in enumerate(
            ((k_in, k_raw), (v_in, kv.at[0, 1, pl.ds(rows, rows), :]), (q_in, q_raw), (out_in, out_raw), (lse_in, lse_raw))
        )
    ]
    for load in loads:
        load.start()
    others = [{"ctx": where, "tp": (tp + i) % ntp} for where in (me, at_y) for i in range(1, ntp)]
    signal_all(
        pltpu.get_barrier_semaphore(), [*along.values(), core_peer, y_peer, cross_peer, *others]
    )

    def shard(d, a):
        if a == 0 or a == half:
            return kv.at[0, :, pl.ds(rows if a == 0 else 0, rows), :]
        return kv.at[a, :, pl.ds(rows if d == 0 else 0, rows), :]

    def pass_on(d, a, from_a, places):
        return send(
            shard(d, from_a), shard(d, a), kv_send.at[d, a], kv_recv.at[d, a], along[places if d == 0 else -places]
        )

    def arrived(a):
        for d in range(2):
            if a <= far[d]:
                pass_on(d, a, a, 1).wait_recv()
            if a + 2 <= far[d]:
                pass_on(d, a + 2, a, 2).start()

    cosine, sine = cos_in[...], sin_in[...]
    loads[0].wait()
    loads[1].wait()
    k = k_raw[...].astype(jnp.float32)
    kv[0, 0, rows : 2 * rows, :] = (k * cosine + pltpu.roll(k, HEAD // 2, 1) * sine).astype(jnp.bfloat16)
    for a in (2, 1):
        for d in range(2):
            if a <= far[d]:
                pass_on(d, a, 0, a).start()

    mine = pl.ds(pl.multiple_of(tp * slab, slab), slab)
    copies = []
    own = None
    for i in range(ntp):
        t = (tp + i) % ntp
        piece = grad_in.at[:, pl.ds(pl.multiple_of(t * width, width), width)]
        for a, where in enumerate((me, at_y)):
            if i == 0 and a == 0:
                own = pltpu.make_async_copy(piece, do_all.at[2, mine, :], local.at[5])
                own.start()
            else:
                slot = 2 if a == 0 else 0
                copies.append(
                    send(piece, do_all.at[slot, mine, :], do_send.at[a, i], do_recv.at[a, i], {"ctx": where, "tp": t})
                )
                copies[-1].start()

    loads[2].wait()
    for h in range(heads):
        at = slice(h * HEAD, (h + 1) * HEAD)
        x = q_raw[:, at].astype(jnp.float32)
        q_all[2, at, :] = (x * cosine + pltpu.roll(x, HEAD // 2, 1) * sine).astype(jnp.bfloat16)
    q_y = send(q_all.at[2], q_all.at[0], q_send.at[0], q_recv.at[0], y_peer)
    q_core = send(q_all.at[2], q_all.at[3], q_send.at[1], q_recv.at[1], core_peer)
    q_y.start()
    q_core.start()

    arrived(1)
    lane = lax.broadcasted_iota(jnp.int32, (1, HEAD), 1)
    dq[...] = jnp.zeros_like(dq)

    def limit_of(block):
        place = map_in[block]
        end = jnp.int32(0)
        for i in range(span_in.shape[0]):
            inside = (place >= span_in[i, 0]) & (place < span_in[i, 1])
            end = end + jnp.where(inside, span_in[i, 1], 0)
        return place * BLK, end * BLK - 1

    for slot, member in enumerate((j + 2 - 4 * yh, (j + 2 - 4 * yh) + 1 - 2 * core, j, j + 1 - 2 * core)):
        pieces = []
        for b in range(2):
            place, end = limit_of((z * QUAD + member) * 2 + b)
            pieces.append(jnp.maximum(place + lane - b * BLK, end))
        limits[slot : slot + 1, :] = jnp.where(lane < BLK, pieces[0], pieces[1])
    for a in range(2, min(4, half - 1)):
        arrived(a)

    def from_slot(slot, axis, i):
        t = (tp - i + ntp) % ntp
        there = do_all.at[slot, pl.ds(pl.multiple_of(t * slab, slab), slab), :]
        return send(there, there, do_send.at[axis, i], do_recv.at[axis, i], core_peer)

    own.wait()
    for i in range(1, ntp):
        from_slot(2, 0, i).wait_recv()
    forward = [send(do_all.at[2], do_all.at[3], fwd_send.at[0], fwd_recv.at[0], core_peer)]
    forward[0].start()
    loads[3].wait()
    loads[4].wait()
    for h in range(heads):
        at = slice(h * HEAD, (h + 1) * HEAD)
        product = do_all[2, :, at].astype(jnp.float32) * out_raw[:, at].astype(jnp.float32)
        stats[2, 0, h : h + 1, :] = lse_raw[h : h + 1, :] * LOG2E
        stats[2, 1, h : h + 1, :] = jnp.sum(product.T, axis=0, keepdims=True)
    small = [
        send(stats.at[2], stats.at[slot], st_send.at[i], st_recv.at[i], peer)
        for i, (slot, peer) in enumerate(((3, core_peer), (0, y_peer), (1, cross_peer)))
    ]
    for copy in small:
        copy.start()
    q_y.wait_recv()
    forward.append(send(q_all.at[0], q_all.at[1], fwd_send.at[1], fwd_recv.at[1], core_peer))
    forward[1].start()
    for a in range(4, half - 1):
        arrived(a)
    for i in range(ntp):
        from_slot(0, 1, i).wait_recv()
    forward.append(send(do_all.at[0], do_all.at[1], fwd_send.at[2], fwd_recv.at[2], core_peer))
    forward[2].start()
    for copy in (q_core, *forward, *small):
        copy.wait_recv()

    sub = lax.broadcasted_iota(jnp.int32, (BLK, HEAD), 0)

    def unit(p, g, keep_part):
        kp, vp = kv[p, 0], kv[p, 1]
        slots = (2 * g, 2 * g + 1)
        qs = jnp.concatenate([q_all[slot] for slot in slots], axis=0)
        grads = jnp.concatenate(
            [do_all[slot, :, h * HEAD : (h + 1) * HEAD] for slot in slots for h in range(heads)], axis=0
        )
        up = (p + half - 1) % half + 1
        shards_z = ((z + up) % nz, (z - p + nz) % nz)
        places = [map_in[(s * QUAD + j) * 2 + b] * BLK for s in shards_z for b in range(2)]
        s = lax.dot_general(kp, qs, (((1,), (1,)), ((), ())), preferred_element_type=jnp.float32)
        dp = lax.dot_general(vp, grads, (((1,), (1,)), ((), ())), preferred_element_type=jnp.float32)
        probs, scores = [], []
        for i, slot in enumerate(slots):
            bound = limits[slot : slot + 1, :]
            allowed = jnp.concatenate([sub <= bound - place for place in places], axis=0)
            for h in range(heads):
                at = slice((i * heads + h) * HEAD, (i * heads + h + 1) * HEAD)
                x = s[:, at] * (scale * LOG2E) - stats[slot, 0, h : h + 1, :]
                prob = jnp.exp2(jnp.where(allowed, x, -jnp.inf))
                probs.append(prob.astype(jnp.bfloat16))
                scores.append((prob * (dp[:, at] - stats[slot, 1, h : h + 1, :])).astype(jnp.bfloat16))
        probs = jnp.concatenate(probs, axis=1)
        scores = jnp.concatenate(scores, axis=1)
        dv = jnp.dot(probs, grads, preferred_element_type=jnp.float32)
        dk = jnp.dot(scores, qs, preferred_element_type=jnp.float32) * scale
        if keep_part:
            part[p, 0] += dk
            part[p, 1] += dv
        else:
            part[p, 0] = dk
            part[p, 1] = dv
        dq[g] += lax.dot_general(scores, kp, (((0,), (0,)), ((), ())), preferred_element_type=jnp.float32)

    def part_of(d, s, p):
        return part[p, :, (0 if d == 0 else rows) : (rows if d == 0 else 2 * rows), :]

    def give(d, s, source, places):
        return send(
            source, carry.at[d, s], rs_send.at[d, s], rs_recv.at[d, s], along[places if d == 0 else -places]
        )

    def start_chain(d, s, p, places):
        at = far[d] - s
        stage[d, at] = part_of(d, s, p).astype(jnp.bfloat16)
        give(d, s, stage.at[d, at], places).start()

    def add_and_give(d, s, p, places):
        give(d, s + 2, carry.at[d, s + 2], 1).wait_recv()
        carry[d, s + 2] = (carry[d, s + 2].astype(jnp.float32) + part_of(d, s, p)).astype(jnp.bfloat16)
        give(d, s, carry.at[d, s + 2], places).start()

    to_core = [send(dq_go.at[i], first.at[i], dq_send.at[i], dq_recv.at[i], core_peer) for i in range(2)]
    span_rows = heads * HEAD

    def one_pair(i, unused):
        p = (half + 1 - i) % half
        s = half + 1 - i

        @pl.when(i == 1)
        def _():
            pass_on(0, half, half, 1).wait_recv()

        if half - 1 > 1:

            @pl.when(i == 2)
            def _():
                arrived(half - 1)

        unit(p, 0, False)

        @pl.when(i == half - 1)
        def _():
            dq_go[0] = (dq[0, span_rows : 2 * span_rows, :] * scale).astype(jnp.bfloat16)
            to_core[0].start()

        unit(p, 1, True)
        for d in range(2):

            @pl.when((i >= 1 + d) & (i <= 2 + d))
            def _():
                start_chain(d, s, p, 2)

            if half > 3 + d:

                @pl.when(i >= 3 + d)
                def _():
                    add_and_give(d, s, p, 2)

        return unused

    lax.fori_loop(0, half, one_pair, 0)
    dq_go[1] = (dq[1, span_rows : 2 * span_rows, :] * scale).astype(jnp.bfloat16)
    to_core[1].start()
    for d in range(2):
        if far[d] >= 3:
            add_and_give(d, 1, 1, 1)
        else:
            start_chain(d, 1, 1, 1)
    to_core[0].wait_recv()
    back[...] = (dq[0, 0:span_rows, :] * scale + first[0].astype(jnp.float32)).astype(jnp.bfloat16)
    to_y = send(back, second, dq_send.at[2], dq_recv.at[2], y_peer)
    to_y.start()
    to_core[1].wait_recv()
    ends = [part[0, what, rows : 2 * rows, :] for what in range(2)]
    for d in range(2):
        for s in (2, 1):
            if s <= far[d]:
                give(d, s, carry.at[d, s], 1).wait_recv()
                ends = [ends[what] + carry[d, s, what].astype(jnp.float32) for what in range(2)]
    gk_out[...] = (ends[0] * cosine - pltpu.roll(ends[0], HEAD // 2, 1) * sine).astype(jnp.bfloat16)
    gv_out[...] = ends[1].astype(jnp.bfloat16)
    to_y.wait_recv()
    for h in range(heads):
        at = slice(h * HEAD, (h + 1) * HEAD)
        x = dq[1, at, :] * scale + first[1, at, :].astype(jnp.float32) + second[at, :].astype(jnp.float32)
        gq_out[:, at] = (x * cosine - pltpu.roll(x, HEAD // 2, 1) * sine).astype(jnp.bfloat16)

    for d in range(2):
        for a in range(1, far[d] + 1):
            pass_on(d, a, 0, 1).wait_send()
            give(d, a, stage.at[d, 0], 1).wait_send()
    for copy in (*copies, q_y, q_core, *forward, *small, *to_core, to_y):
        copy.wait_send()


def shards(queries, keys, values, attn_out, out_grad, logsumexp, position_ids, block_map, span_blocks):
    rows, width = queries.shape
    heads = width // HEAD
    nz = lax.axis_size("ctx") // QUAD
    ntp = lax.axis_size("tp")
    cosine, sine = rope_tables(position_ids)
    vmem = pl.BlockSpec(memory_space=pltpu.VMEM)
    smem = pl.BlockSpec(memory_space=pltpu.SMEM)
    hbm = pl.BlockSpec(memory_space=pl.ANY)
    dma = pltpu.SemaphoreType.DMA
    bf16, f32 = jnp.bfloat16, jnp.float32
    half = nz // 2
    tall = heads * HEAD
    return pl.pallas_call(
        functools.partial(step_kernel, nz, ntp),
        out_shape=(
            jax.ShapeDtypeStruct((rows, width), bf16),
            jax.ShapeDtypeStruct((rows, HEAD), bf16),
            jax.ShapeDtypeStruct((rows, HEAD), bf16),
        ),
        in_specs=[smem, smem, hbm, hbm, hbm, hbm, hbm, hbm, vmem, vmem],
        out_specs=(vmem, vmem, vmem),
        scratch_shapes=[
            pltpu.VMEM((rows, width), bf16),
            pltpu.VMEM((rows, width), bf16),
            pltpu.VMEM((heads, rows), f32),
            pltpu.VMEM((rows, HEAD), bf16),
            pltpu.VMEM((QUAD, tall, HEAD), bf16),
            pltpu.VMEM((QUAD, rows, width), bf16),
            pltpu.VMEM((QUAD, 2, heads, rows), f32),
            pltpu.VMEM((half, 2, 2 * rows, HEAD), bf16),
            pltpu.VMEM((half, 2, 2 * rows, HEAD), f32),
            pltpu.VMEM((2, 2 * tall, HEAD), f32),
            pltpu.VMEM((2, tall, HEAD), bf16),
            pltpu.VMEM((2, tall, HEAD), bf16),
            pltpu.VMEM((tall, HEAD), bf16),
            pltpu.VMEM((2, half + 1, 2, rows, HEAD), bf16),
            pltpu.VMEM((2, 2, 2, rows, HEAD), bf16),
            pltpu.VMEM((tall, HEAD), bf16),
            pltpu.VMEM((8, HEAD), jnp.int32),
            dma((6,)), dma((2, ntp)), dma((2, ntp)), dma((2, half + 1)), dma((2, half + 1)),
            dma((2,)), dma((2,)), dma((3,)), dma((3,)), dma((3,)), dma((3,)),
            dma((2, half + 1)), dma((2, half + 1)), dma((3,)), dma((3,)),
        ],
        compiler_params=pltpu.CompilerParams(
            vmem_limit_bytes=56 * 1024 * 1024, collective_id=0, has_side_effects=True
        ),
        name="attention_backward",
    )(
        block_map, span_blocks, queries, keys, values, attn_out, out_grad, logsumexp, cosine, sine
    )


def solution(mesh):
    return jax.shard_map(
        shards,
        mesh=mesh,
        in_specs=(
            P("ctx", "tp"),
            P("ctx", "tp"),
            P("ctx", "tp"),
            P("ctx", "tp"),
            P(("ctx", "tp"), None),
            P("tp", "ctx"),
            P(None, "ctx"),
            P(),
            P(),
        ),
        out_specs=(P("ctx", "tp"), P("ctx", "tp"), P("ctx", "tp")),
        check_vma=False,
    )
```

time: 301 us -> 84.9 us (0.28)
  the two profiles are of different devices: /device:TPU:2 before, /device:TPU:1 now
where the time goes in v3:
time: 84.9 us; the launch traced here: 83.8 us
  Pallas kernels  77 us (91%)
  local copies, waits for them, and re-layouts  5.1 us (6%)
  other arithmetic  1.02 us (1%)
    pallas_call x1, Pallas kernels, shards(): pl.pallas_call(functools.partial(step_kernel, nz, ntp), out_shape=(jax.Sh...  77 us
    unnamed x12, local copies, waits for them, and re-layouts  5.1 us

profile of v3, /device:TPU:1, one launch (start us, length us, event | category | flops | bytes accessed | tf_op | source)
XLA Modules:
  0.0 83.8 jit_solution(15288891581770660484)
XLA Ops:
  0.7 0.0 copy-start.2
  0.7 0.7 copy-done.2
  1.3 0.0 copy-start.3
  1.3 0.7 copy-done.3
  2.0 0.7 copy.12.span_in
  2.7 1.0 %sine_multiply_fusion = (f32[128,128]{1,0:T(8,128)}, f32[128,128]{1,0:T(8,128)}) fusion(f32[128]{0:T(128)S(1)} %get-tuple-element.8, f32[128]{0:T(128)S(1)} %get-tuple-element.9, s32[128]{0:T(128)S(1)} %get-tuple-element.6, s32[128]{0:T(128)S(1)} %get-tuple-element.7, s32[128]{0:T(128)S(1)} %get-tuple-element.5, pred[128]{0:T(512)(128)(4,1)S(1)} %get-tuple-element.10, ...), kind=kLoop, calls=%fused_computation | loop fusion | flops 81920 | bytes 133888 | tf_op jit(solution)/shard_map/mul | solution.py:31
  3.7 77.0 %attention_backward.1 = (bf16[128,1024]{1,0:T(8,128)(2,1)}, bf16[128,128]{1,0:T(8,128)(2,1)}, bf16[128,128]{1,0:T(8,128)(2,1)}) custom-call(s32[128]{0:T(128)} %map_in.1, s32[16,2]{1,0:T(8,128)} %copy.12.span_in, bf16[128,1024]{1,0:T(8,128)(2,1)} %q_in.1, bf16[128,128]{1,0:T(8,128)(2,1)} %k_in.1, bf16[128,128]{1,0:T(8,128)(2,1)} %v_in.1, ...), custom_call_target="tpu_custom_call" | custom-call | tf_op jit(solution)/shard_map/attention_backward/pallas_call | solution.py:343
  80.7 0.0 copy-start.1
  80.7 1.7 %copy.16 = bf16[128,1024]{1,0:T(8,128)(2,1)} copy(bf16[128,1024]{1,0:T(8,128)(2,1)} %get-tuple-element.15) | data formatting | bytes 524288
  82.4 0.0 copy-done.1
  82.4 0.0 copy-start
  82.4 0.6 copy.17
  83.0 0.2 copy-done
  83.2 0.6 copy.18
  (3 shorter events, 0.0 us)
Async XLA Ops:
  0.7 0.7 copy-start.2
  1.3 0.7 copy-start.3
  80.7 1.7 %copy-start.1 = (bf16[128,128]{1,0:T(8,128)(2,1)S(1)}, bf16[128,128]{1,0:T(8,128)(2,1)}, u32[]{:S(2)}) copy-start(bf16[128,128]{1,0:T(8,128)(2,1)} %get-tuple-element.16) | copy-start | bytes 98308
  82.4 0.8 copy-start

commit v4 on v3

--- a/solution.py
+++ b/solution.py
@@ -15,20 +15,16 @@
 LOG2E = 1.4426950408889634
 
 
-def rope_tables(position_ids):
+def rope_tables(ids):
     half = HEAD // 2
-    pair = jnp.arange(HEAD, dtype=jnp.int32) % half
+    pair = lax.broadcasted_iota(jnp.int32, (half, HEAD), 0)
     inverse = jnp.exp(pair.astype(jnp.float32) * jnp.float32(-2.0 * math.log(THETA) / HEAD))
     first_cut = HEAD // 8
     second_cut = first_cut + 3 * HEAD // 16
-    picked = jnp.where(
-        pair[None, :] < first_cut,
-        position_ids[0][:, None],
-        jnp.where(pair[None, :] < second_cut, position_ids[1][:, None], position_ids[2][:, None]),
-    )
-    angles = picked.astype(jnp.float32) * inverse[None, :]
-    sign = jnp.where(jnp.arange(HEAD) < half, -1.0, 1.0).astype(jnp.float32)
-    return jnp.cos(angles), jnp.sin(angles) * sign[None, :]
+    picked = jnp.where(pair < first_cut, ids[0:1, :], jnp.where(pair < second_cut, ids[1:2, :], ids[2:3, :]))
+    angles = picked.astype(jnp.float32) * inverse
+    cosine, sine = jnp.cos(angles), jnp.sin(angles)
+    return jnp.concatenate([cosine, cosine], axis=0).T, jnp.concatenate([-sine, sine], axis=0).T
 
 
 MESH = pl.DeviceIdType.MESH
@@ -52,8 +48,8 @@
 
 
 def step_kernel(
-    nz, ntp, map_in, span_in, q_in, k_in, v_in, out_in, grad_in, lse_in, cos_in, sin_in,
-    gq_out, gk_out, gv_out,
+    nz, ntp, map_in, span_in, q_in, k_in, v_in, out_in, grad_in, lse_in, ids_in,
+    all_out,
     q_raw, out_raw, lse_raw, k_raw, q_all, do_all, stats, kv, part, dq, dq_go, first, second, carry, stage, back, limits,
     local, do_send, do_recv, kv_send, kv_recv, q_send, q_recv, fwd_send, fwd_recv, st_send, st_recv,
     rs_send, rs_recv, dq_send, dq_recv,
@@ -62,7 +58,7 @@
     tp = lax.axis_index("tp")
     z, j = me // QUAD, me % QUAD
     yh, core = j // 2, j % 2
-    rows, width = gq_out.shape
+    rows, width = q_in.shape
     heads = width // HEAD
     slab = rows // ntp
     n = nz * QUAD
@@ -84,6 +80,7 @@
     ]
     for load in loads:
         load.start()
+    cosine, sine = rope_tables(ids_in)
     others = [{"ctx": where, "tp": (tp + i) % ntp} for where in (me, at_y) for i in range(1, ntp)]
     signal_all(
         pltpu.get_barrier_semaphore(), [*along.values(), core_peer, y_peer, cross_peer, *others]
@@ -106,7 +103,6 @@
             if a + 2 <= far[d]:
                 pass_on(d, a + 2, a, 2).start()
 
-    cosine, sine = cos_in[...], sin_in[...]
     loads[0].wait()
     loads[1].wait()
     k = k_raw[...].astype(jnp.float32)
@@ -143,16 +139,15 @@
     q_y.start()
     q_core.start()
 
-    arrived(1)
     lane = lax.broadcasted_iota(jnp.int32, (1, HEAD), 1)
     dq[...] = jnp.zeros_like(dq)
 
     def limit_of(block):
         place = map_in[block]
         end = jnp.int32(0)
-        for i in range(span_in.shape[0]):
-            inside = (place >= span_in[i, 0]) & (place < span_in[i, 1])
-            end = end + jnp.where(inside, span_in[i, 1], 0)
+        for i in range(span_in.shape[1]):
+            inside = (place >= span_in[0, i]) & (place < span_in[1, i])
+            end = end + jnp.where(inside, span_in[1, i], 0)
         return place * BLK, end * BLK - 1
 
     for slot, member in enumerate((j + 2 - 4 * yh, (j + 2 - 4 * yh) + 1 - 2 * core, j, j + 1 - 2 * core)):
@@ -161,6 +156,7 @@
             place, end = limit_of((z * QUAD + member) * 2 + b)
             pieces.append(jnp.maximum(place + lane - b * BLK, end))
         limits[slot : slot + 1, :] = jnp.where(lane < BLK, pieces[0], pieces[1])
+    arrived(1)
     for a in range(2, min(4, half - 1)):
         arrived(a)
 
@@ -255,18 +251,20 @@
 
     to_core = [send(dq_go.at[i], first.at[i], dq_send.at[i], dq_recv.at[i], core_peer) for i in range(2)]
     span_rows = heads * HEAD
+    near = 2 if half >= 4 else 1
 
     def one_pair(i, unused):
-        p = (half + 1 - i) % half
-        s = half + 1 - i
-
-        @pl.when(i == 1)
+        late = (i + half - near) // half
+        s = half + near - i
+        p = (1 - late) * (i + 1) + late * (s % half)
+
+        @pl.when(i == near)
         def _():
             pass_on(0, half, half, 1).wait_recv()
 
         if half - 1 > 1:
 
-            @pl.when(i == 2)
+            @pl.when(i == near + 1)
             def _():
                 arrived(half - 1)
 
@@ -280,13 +278,13 @@
         unit(p, 1, True)
         for d in range(2):
 
-            @pl.when((i >= 1 + d) & (i <= 2 + d))
+            @pl.when((i >= near + d) & (i <= near + 1 + d))
             def _():
                 start_chain(d, s, p, 2)
 
-            if half > 3 + d:
-
-                @pl.when(i >= 3 + d)
+            if half > near + 2 + d:
+
+                @pl.when(i >= near + 2 + d)
                 def _():
                     add_and_give(d, s, p, 2)
 
@@ -295,15 +293,16 @@
     lax.fori_loop(0, half, one_pair, 0)
     dq_go[1] = (dq[1, span_rows : 2 * span_rows, :] * scale).astype(jnp.bfloat16)
     to_core[1].start()
-    for d in range(2):
-        if far[d] >= 3:
-            add_and_give(d, 1, 1, 1)
-        else:
-            start_chain(d, 1, 1, 1)
     to_core[0].wait_recv()
     back[...] = (dq[0, 0:span_rows, :] * scale + first[0].astype(jnp.float32)).astype(jnp.bfloat16)
     to_y = send(back, second, dq_send.at[2], dq_recv.at[2], y_peer)
     to_y.start()
+    for s in range(near, 0, -1):
+        for d in range(2):
+            if s + 2 <= far[d]:
+                add_and_give(d, s, s, min(s, 2))
+            elif s <= far[d]:
+                start_chain(d, s, s, min(s, 2))
     to_core[1].wait_recv()
     ends = [part[0, what, rows : 2 * rows, :] for what in range(2)]
     for d in range(2):
@@ -311,13 +310,13 @@
             if s <= far[d]:
                 give(d, s, carry.at[d, s], 1).wait_recv()
                 ends = [ends[what] + carry[d, s, what].astype(jnp.float32) for what in range(2)]
-    gk_out[...] = (ends[0] * cosine - pltpu.roll(ends[0], HEAD // 2, 1) * sine).astype(jnp.bfloat16)
-    gv_out[...] = ends[1].astype(jnp.bfloat16)
+    all_out[:, width : width + HEAD] = (ends[0] * cosine - pltpu.roll(ends[0], HEAD // 2, 1) * sine).astype(jnp.bfloat16)
+    all_out[:, width + HEAD :] = ends[1].astype(jnp.bfloat16)
     to_y.wait_recv()
     for h in range(heads):
         at = slice(h * HEAD, (h + 1) * HEAD)
         x = dq[1, at, :] * scale + first[1, at, :].astype(jnp.float32) + second[at, :].astype(jnp.float32)
-        gq_out[:, at] = (x * cosine - pltpu.roll(x, HEAD // 2, 1) * sine).astype(jnp.bfloat16)
+        all_out[:, at] = (x * cosine - pltpu.roll(x, HEAD // 2, 1) * sine).astype(jnp.bfloat16)
 
     for d in range(2):
         for a in range(1, far[d] + 1):
@@ -332,7 +331,6 @@
     heads = width // HEAD
     nz = lax.axis_size("ctx") // QUAD
     ntp = lax.axis_size("tp")
-    cosine, sine = rope_tables(position_ids)
     vmem = pl.BlockSpec(memory_space=pltpu.VMEM)
     smem = pl.BlockSpec(memory_space=pltpu.SMEM)
     hbm = pl.BlockSpec(memory_space=pl.ANY)
@@ -340,15 +338,11 @@
     bf16, f32 = jnp.bfloat16, jnp.float32
     half = nz // 2
     tall = heads * HEAD
-    return pl.pallas_call(
+    together = pl.pallas_call(
         functools.partial(step_kernel, nz, ntp),
-        out_shape=(
-            jax.ShapeDtypeStruct((rows, width), bf16),
-            jax.ShapeDtypeStruct((rows, HEAD), bf16),
-            jax.ShapeDtypeStruct((rows, HEAD), bf16),
-        ),
-        in_specs=[smem, smem, hbm, hbm, hbm, hbm, hbm, hbm, vmem, vmem],
-        out_specs=(vmem, vmem, vmem),
+        out_shape=jax.ShapeDtypeStruct((rows, width + 2 * HEAD), bf16),
+        in_specs=[smem, smem, hbm, hbm, hbm, hbm, hbm, hbm, vmem],
+        out_specs=vmem,
         scratch_shapes=[
             pltpu.VMEM((rows, width), bf16),
             pltpu.VMEM((rows, width), bf16),
@@ -376,8 +370,9 @@
         ),
         name="attention_backward",
     )(
-        block_map, span_blocks, queries, keys, values, attn_out, out_grad, logsumexp, cosine, sine
+        block_map, span_blocks.T, queries, keys, values, attn_out, out_grad, logsumexp, position_ids
     )
+    return together[:, :width], together[:, width : width + HEAD], together[:, width + HEAD :]
 
 
 def solution(mesh):

time: 84.9 us -> 82.8 us (0.975); the launches traced: 83.8 us -> 82.6 us
  local copies, waits for them, and re-layouts: 5.1 us -> 3.07 us
  Pallas kernels: 77 us -> 78.9 us
  other arithmetic: 1.02 us -> 0 us
    unnamed x12 -> x0, local copies, waits for them, and re-layouts: 5.1 us -> none
    slice x0 -> x2, local copies, waits for them, and re-layouts: none -> 3.07 us  [the longest x1 1.67 us: shards(): together[:, :width]]
    pallas_call x1, Pallas kernels: 77 us -> 78.9 us  [shards(): pl.pallas_call(functools.partial(step_kernel, nz, ntp), out_shape=jax.Sha...]
    mul x1 -> x0, other arithmetic: 1 us -> none  [rope_tables(): return (jnp.cos(angles), jnp.sin(angles) * sign[None, :])]
where the time goes in v4:
time: 82.8 us; the launch traced here: 82.6 us
  Pallas kernels  78.9 us (95%)
  local copies, waits for them, and re-layouts  3.07 us (4%)
    pallas_call x1, Pallas kernels, shards(): pl.pallas_call(functools.partial(step_kernel, nz, ntp), out_shape=jax.Sha...  78.9 us
    slice x1, local copies, waits for them, and re-layouts, shards(): together[:, :width]  1.67 us

profile of v4, /device:TPU:1, one launch (start us, length us, event | category | flops | bytes accessed | tf_op | source)
XLA Modules:
  0.0 82.6 jit_solution(16258673566005995873)
XLA Ops:
  0.6 78.9 %attention_backward.1 = bf16[128,1280]{1,0:T(8,128)(2,1)} custom-call(s32[128]{0:T(128)} %map_in.1, s32[2,16]{1,0:T(2,128)} %bitcast.1, bf16[128,1024]{1,0:T(8,128)(2,1)} %q_in.1, bf16[128,128]{1,0:T(8,128)(2,1)} %k_in.1, bf16[128,128]{1,0:T(8,128)(2,1)} %v_in.1, bf16[128,1024]{1,0:T(8,128)(2,1)} %out_in.1, bf16[16,8192]{1,0:T(8,128)(2,1)} %grad_in.1, ...), custom_call_target="tpu_custom_call" | custom-call | tf_op jit(solution)/shard_map/attention_backward/pallas_call | solution.py:341
  79.5 1.4 %fusion = (bf16[128,128]{1,0:T(8,128)(2,1)}, bf16[128,128]{1,0:T(8,128)(2,1)}) fusion(bf16[128,1280]{1,0:T(8,128)(2,1)} %attention_backward.1), kind=kLoop, calls=%fused_computation | loop fusion | bytes 131072 | tf_op jit(solution)/shard_map/slice | solution.py:375
  80.9 1.7 %slice.9 = bf16[128,1024]{1,0:T(8,128)(2,1)} slice(bf16[128,1280]{1,0:T(8,128)(2,1)} %attention_backward.1), slice={[0:128], [0:1024]} | slice | bytes 524288 | tf_op jit(solution)/shard_map/slice | solution.py:375

commit v5 on v4

--- a/solution.py
+++ b/solution.py
@@ -33,7 +33,6 @@
 def signal_all(barrier, peers):
     for peer in peers:
         pl.semaphore_signal(barrier, inc=1, device_id=peer, device_id_type=MESH)
-    pl.semaphore_wait(barrier, len(peers))
 
 
 def send(source, target, send_sem, recv_sem, peer):
@@ -80,11 +79,30 @@
     ]
     for load in loads:
         load.start()
+    others = [{"ctx": where, "tp": (tp + i) % ntp} for where in (me, at_y) for i in range(1, ntp)]
+    peers = [*along.values(), core_peer, y_peer, cross_peer, *others]
+    barrier = pltpu.get_barrier_semaphore()
+    signal_all(barrier, peers)
     cosine, sine = rope_tables(ids_in)
-    others = [{"ctx": where, "tp": (tp + i) % ntp} for where in (me, at_y) for i in range(1, ntp)]
-    signal_all(
-        pltpu.get_barrier_semaphore(), [*along.values(), core_peer, y_peer, cross_peer, *others]
-    )
+    lane = lax.broadcasted_iota(jnp.int32, (1, HEAD), 1)
+    dq[...] = jnp.zeros_like(dq)
+    part[...] = jnp.zeros_like(part)
+
+    def limit_of(block):
+        place = map_in[block]
+        end = jnp.int32(0)
+        for i in range(span_in.shape[1]):
+            inside = (place >= span_in[0, i]) & (place < span_in[1, i])
+            end = end + jnp.where(inside, span_in[1, i], 0)
+        return place * BLK, end * BLK - 1
+
+    for slot, member in enumerate((j + 2 - 4 * yh, (j + 2 - 4 * yh) + 1 - 2 * core, j, j + 1 - 2 * core)):
+        pieces = []
+        for b in range(2):
+            place, end = limit_of((z * QUAD + member) * 2 + b)
+            pieces.append(jnp.maximum(place + lane - b * BLK, end))
+        limits[slot] = jnp.where(lane < BLK, pieces[0], pieces[1])
+    pl.semaphore_wait(barrier, len(peers))
 
     def shard(d, a):
         if a == 0 or a == half:
@@ -139,26 +157,11 @@
     q_y.start()
     q_core.start()
 
-    lane = lax.broadcasted_iota(jnp.int32, (1, HEAD), 1)
-    dq[...] = jnp.zeros_like(dq)
-
-    def limit_of(block):
-        place = map_in[block]
-        end = jnp.int32(0)
-        for i in range(span_in.shape[1]):
-            inside = (place >= span_in[0, i]) & (place < span_in[1, i])
-            end = end + jnp.where(inside, span_in[1, i], 0)
-        return place * BLK, end * BLK - 1
-
-    for slot, member in enumerate((j + 2 - 4 * yh, (j + 2 - 4 * yh) + 1 - 2 * core, j, j + 1 - 2 * core)):
-        pieces = []
-        for b in range(2):
-            place, end = limit_of((z * QUAD + member) * 2 + b)
-            pieces.append(jnp.maximum(place + lane - b * BLK, end))
-        limits[slot : slot + 1, :] = jnp.where(lane < BLK, pieces[0], pieces[1])
     arrived(1)
-    for a in range(2, min(4, half - 1)):
+    near = 3 if half >= 8 else (2 if half >= 4 else 1)
+    for a in range(2, near + 1):
         arrived(a)
+    later = list(range(near + 1, half - 1))
 
     def from_slot(slot, axis, i):
         t = (tp - i + ntp) % ntp
@@ -186,18 +189,15 @@
     q_y.wait_recv()
     forward.append(send(q_all.at[0], q_all.at[1], fwd_send.at[1], fwd_recv.at[1], core_peer))
     forward[1].start()
-    for a in range(4, half - 1):
-        arrived(a)
-    for i in range(ntp):
-        from_slot(0, 1, i).wait_recv()
+    if later:
+        arrived(later[0])
     forward.append(send(do_all.at[0], do_all.at[1], fwd_send.at[2], fwd_recv.at[2], core_peer))
-    forward[2].start()
-    for copy in (q_core, *forward, *small):
+    for copy in (q_core, forward[0], small[0]):
         copy.wait_recv()
 
     sub = lax.broadcasted_iota(jnp.int32, (BLK, HEAD), 0)
 
-    def unit(p, g, keep_part):
+    def unit(p, g):
         kp, vp = kv[p, 0], kv[p, 1]
         slots = (2 * g, 2 * g + 1)
         qs = jnp.concatenate([q_all[slot] for slot in slots], axis=0)
@@ -211,7 +211,7 @@
         dp = lax.dot_general(vp, grads, (((1,), (1,)), ((), ())), preferred_element_type=jnp.float32)
         probs, scores = [], []
         for i, slot in enumerate(slots):
-            bound = limits[slot : slot + 1, :]
+            bound = limits[slot]
             allowed = jnp.concatenate([sub <= bound - place for place in places], axis=0)
             for h in range(heads):
                 at = slice((i * heads + h) * HEAD, (i * heads + h + 1) * HEAD)
@@ -223,12 +223,8 @@
         scores = jnp.concatenate(scores, axis=1)
         dv = jnp.dot(probs, grads, preferred_element_type=jnp.float32)
         dk = jnp.dot(scores, qs, preferred_element_type=jnp.float32) * scale
-        if keep_part:
-            part[p, 0] += dk
-            part[p, 1] += dv
-        else:
-            part[p, 0] = dk
-            part[p, 1] = dv
+        part[p, 0] += dk
+        part[p, 1] += dv
         dq[g] += lax.dot_general(scores, kp, (((0,), (0,)), ((), ())), preferred_element_type=jnp.float32)
 
     def part_of(d, s, p):
@@ -251,46 +247,66 @@
 
     to_core = [send(dq_go.at[i], first.at[i], dq_send.at[i], dq_recv.at[i], core_peer) for i in range(2)]
     span_rows = heads * HEAD
-    near = 2 if half >= 4 else 1
-
-    def one_pair(i, unused):
-        late = (i + half - near) // half
-        s = half + near - i
-        p = (1 - late) * (i + 1) + late * (s % half)
-
-        @pl.when(i == near)
+
+    def one_unit(u, unused):
+        late = (u + 2 * half - 2 * near) // (2 * half)
+        order = (u + 2 * half - 2 * near) % (2 * half) // 2
+        s = half - order
+        p = (1 - late) * (u % near + 1) + late * (s % half)
+        g = (1 - late) * (1 - u // near % 2) + late * (u % 2)
+
+        @pl.when(u == 2 * near)
         def _():
             pass_on(0, half, half, 1).wait_recv()
 
-        if half - 1 > 1:
-
-            @pl.when(i == near + 1)
+        if half - 1 > near:
+
+            @pl.when(u == 2 * near + 2)
             def _():
                 arrived(half - 1)
 
-        unit(p, 0, False)
-
-        @pl.when(i == half - 1)
+        unit(p, g)
+
+        @pl.when(u == 0)
+        def _():
+            if len(later) > 1:
+                arrived(later[1])
+            for i in range(ntp):
+                from_slot(0, 1, i).wait_recv()
+            forward[2].start()
+
+        if len(later) > 2:
+
+            @pl.when(u == 1)
+            def _():
+                arrived(later[2])
+
+        @pl.when(u == near - 1)
+        def _():
+            for copy in (*forward[1:], *small[1:]):
+                copy.wait_recv()
+
+        @pl.when(u == 2 * half - 2)
         def _():
             dq_go[0] = (dq[0, span_rows : 2 * span_rows, :] * scale).astype(jnp.bfloat16)
             to_core[0].start()
 
-        unit(p, 1, True)
         for d in range(2):
-
-            @pl.when((i >= near + d) & (i <= near + 1 + d))
+            first_of = 2 * near + 2 * d + 1
+
+            @pl.when((u == first_of) | (u == first_of + 2))
             def _():
                 start_chain(d, s, p, 2)
 
-            if half > near + 2 + d:
-
-                @pl.when(i >= near + 2 + d)
+            if 2 * half > first_of + 4:
+
+                @pl.when((u >= first_of + 4) & (u % 2 == 1))
                 def _():
                     add_and_give(d, s, p, 2)
 
         return unused
 
-    lax.fori_loop(0, half, one_pair, 0)
+    lax.fori_loop(0, 2 * half, one_unit, 0)
     dq_go[1] = (dq[1, span_rows : 2 * span_rows, :] * scale).astype(jnp.bfloat16)
     to_core[1].start()
     to_core[0].wait_recv()
@@ -360,7 +376,7 @@
             pltpu.VMEM((2, half + 1, 2, rows, HEAD), bf16),
             pltpu.VMEM((2, 2, 2, rows, HEAD), bf16),
             pltpu.VMEM((tall, HEAD), bf16),
-            pltpu.VMEM((8, HEAD), jnp.int32),
+            pltpu.VMEM((QUAD, 1, HEAD), jnp.int32),
             dma((6,)), dma((2, ntp)), dma((2, ntp)), dma((2, half + 1)), dma((2, half + 1)),
             dma((2,)), dma((2,)), dma((3,)), dma((3,)), dma((3,)), dma((3,)),
             dma((2, half + 1)), dma((2, half + 1)), dma((3,)), dma((3,)),

time: 82.8 us -> 80.3 us (0.970); the launches traced: 82.6 us -> 79.2 us
  Pallas kernels: 78.9 us -> 75.5 us
    pallas_call x1, Pallas kernels: 78.9 us -> 75.5 us  [shards(): pl.pallas_call(functools.partial(step_kernel, nz, ntp), out_shape=jax.Sha...]
where the time goes in v5:
time: 80.3 us; the launch traced here: 79.2 us
  Pallas kernels  75.5 us (94%)
  local copies, waits for them, and re-layouts  3.07 us (4%)
    pallas_call x1, Pallas kernels, shards(): pl.pallas_call(functools.partial(step_kernel, nz, ntp), out_shape=jax.Sha...  75.5 us
    slice x1, local copies, waits for them, and re-layouts, shards(): together[:, :width]  1.67 us

profile of v5, /device:TPU:1, one launch (start us, length us, event | category | flops | bytes accessed | tf_op | source)
XLA Modules:
  0.0 79.2 jit_solution(191486208318290529)
XLA Ops:
  0.6 75.5 %attention_backward.1 = bf16[128,1280]{1,0:T(8,128)(2,1)} custom-call(s32[128]{0:T(128)} %map_in.1, s32[2,16]{1,0:T(2,128)} %bitcast.1, bf16[128,1024]{1,0:T(8,128)(2,1)} %q_in.1, bf16[128,128]{1,0:T(8,128)(2,1)} %k_in.1, bf16[128,128]{1,0:T(8,128)(2,1)} %v_in.1, bf16[128,1024]{1,0:T(8,128)(2,1)} %out_in.1, bf16[16,8192]{1,0:T(8,128)(2,1)} %grad_in.1, ...), custom_call_target="tpu_custom_call" | custom-call | tf_op jit(solution)/shard_map/attention_backward/pallas_call | solution.py:357
  76.2 1.4 %fusion = (bf16[128,128]{1,0:T(8,128)(2,1)}, bf16[128,128]{1,0:T(8,128)(2,1)}) fusion(bf16[128,1280]{1,0:T(8,128)(2,1)} %attention_backward.1), kind=kLoop, calls=%fused_computation | loop fusion | bytes 131072 | tf_op jit(solution)/shard_map/slice | solution.py:391
  77.6 1.7 %slice.9 = bf16[128,1024]{1,0:T(8,128)(2,1)} slice(bf16[128,1280]{1,0:T(8,128)(2,1)} %attention_backward.1), slice={[0:128], [0:1024]} | slice | bytes 524288 | tf_op jit(solution)/shard_map/slice | solution.py:391

commit v6 on v5

--- a/solution.py
+++ b/solution.py
@@ -69,7 +69,8 @@
     core_peer = {"ctx": at_core, "tp": tp}
     y_peer = {"ctx": at_y, "tp": tp}
     cross_peer = {"ctx": at_core + 2 - 4 * yh, "tp": tp}
-    along = {k: {"ctx": (me + QUAD * k + n) % n, "tp": tp} for k in (1, 2, -1, -2)}
+    near = 3 if half >= 8 else 2
+    along = {k: {"ctx": (me + QUAD * k + n) % n, "tp": tp} for i in range(1, near + 3) for k in (i, -i)}
 
     loads = [
         pltpu.make_async_copy(source, target, local.at[i])
@@ -158,7 +159,6 @@
     q_core.start()
 
     arrived(1)
-    near = 3 if half >= 8 else (2 if half >= 4 else 1)
     for a in range(2, near + 1):
         arrived(a)
     later = list(range(near + 1, half - 1))
@@ -236,9 +236,8 @@
         )
 
     def start_chain(d, s, p, places):
-        at = far[d] - s
-        stage[d, at] = part_of(d, s, p).astype(jnp.bfloat16)
-        give(d, s, stage.at[d, at], places).start()
+        stage[d, s] = part_of(d, s, p).astype(jnp.bfloat16)
+        give(d, s, stage.at[d, s], places).start()
 
     def add_and_give(d, s, p, places):
         give(d, s + 2, carry.at[d, s + 2], 1).wait_recv()
@@ -246,14 +245,17 @@
         give(d, s, carry.at[d, s + 2], places).start()
 
     to_core = [send(dq_go.at[i], first.at[i], dq_send.at[i], dq_recv.at[i], core_peer) for i in range(2)]
+    to_y = send(back, second, dq_send.at[2], dq_recv.at[2], y_peer)
     span_rows = heads * HEAD
 
     def one_unit(u, unused):
         late = (u + 2 * half - 2 * near) // (2 * half)
+        last = (u + 4) // (2 * half)
         order = (u + 2 * half - 2 * near) % (2 * half) // 2
+        order = (1 - last) * order + last * (half - near - 2 + u % 2)
         s = half - order
         p = (1 - late) * (u % near + 1) + late * (s % half)
-        g = (1 - late) * (1 - u // near % 2) + late * (u % 2)
+        g = (1 - late) * (1 - u // near % 2) + late * ((1 - last) * (u % 2) + last * (u % 4 // 2))
 
         @pl.when(u == 2 * near)
         def _():
@@ -286,43 +288,44 @@
             for copy in (*forward[1:], *small[1:]):
                 copy.wait_recv()
 
-        @pl.when(u == 2 * half - 2)
+        @pl.when(u == 2 * half - 3)
         def _():
             dq_go[0] = (dq[0, span_rows : 2 * span_rows, :] * scale).astype(jnp.bfloat16)
             to_core[0].start()
 
-        for d in range(2):
-            first_of = 2 * near + 2 * d + 1
-
-            @pl.when((u == first_of) | (u == first_of + 2))
+        for order_of in range(half - near):
+            place = half - order_of
+            ends = 2 * half - 2 + order_of - (half - near - 2)
+            done = ends if order_of >= half - near - 2 else 2 * (near + order_of) + 1
+
+            @pl.when(u == done)
             def _():
-                start_chain(d, s, p, 2)
-
-            if 2 * half > first_of + 4:
-
-                @pl.when((u >= first_of + 4) & (u % 2 == 1))
-                def _():
-                    add_and_give(d, s, p, 2)
+                for d in range(2):
+                    places = 2 if place - 2 > near else place
+                    if place + 2 <= far[d]:
+                        add_and_give(d, place, place % half, places)
+                    elif place <= far[d]:
+                        start_chain(d, place, place % half, places)
+                if order_of == 0:
+                    for a in range(1, near + 1):
+                        for d in range(2):
+                            start_chain(d, a, a, a)
+
+        @pl.when(u == 2 * half - 2)
+        def _():
+            to_core[0].wait_recv()
+            back[...] = (dq[0, 0:span_rows, :] * scale + first[0].astype(jnp.float32)).astype(jnp.bfloat16)
+            to_y.start()
 
         return unused
 
     lax.fori_loop(0, 2 * half, one_unit, 0)
     dq_go[1] = (dq[1, span_rows : 2 * span_rows, :] * scale).astype(jnp.bfloat16)
     to_core[1].start()
-    to_core[0].wait_recv()
-    back[...] = (dq[0, 0:span_rows, :] * scale + first[0].astype(jnp.float32)).astype(jnp.bfloat16)
-    to_y = send(back, second, dq_send.at[2], dq_recv.at[2], y_peer)
-    to_y.start()
-    for s in range(near, 0, -1):
-        for d in range(2):
-            if s + 2 <= far[d]:
-                add_and_give(d, s, s, min(s, 2))
-            elif s <= far[d]:
-                start_chain(d, s, s, min(s, 2))
     to_core[1].wait_recv()
     ends = [part[0, what, rows : 2 * rows, :] for what in range(2)]
     for d in range(2):
-        for s in (2, 1):
+        for s in range(1, near + 3):
             if s <= far[d]:
                 give(d, s, carry.at[d, s], 1).wait_recv()
                 ends = [ends[what] + carry[d, s, what].astype(jnp.float32) for what in range(2)]
@@ -340,6 +343,18 @@
             give(d, a, stage.at[d, 0], 1).wait_send()
     for copy in (*copies, q_y, q_core, *forward, *small, *to_core, to_y):
         copy.wait_send()
+
+
+def divide_kernel(together, gq_out, gk_out, gv_out, done):
+    width = gq_out.shape[1]
+    copies = [
+        pltpu.make_async_copy(together.at[:, pl.ds(start, out.shape[1])], out, done.at[i])
+        for i, (start, out) in enumerate(((0, gq_out), (width, gk_out), (width + HEAD, gv_out)))
+    ]
+    for copy in copies:
+        copy.start()
+    for copy in copies:
+        copy.wait()
 
 
 def shards(queries, keys, values, attn_out, out_grad, logsumexp, position_ids, block_map, span_blocks):
@@ -374,7 +389,7 @@
             pltpu.VMEM((2, tall, HEAD), bf16),
             pltpu.VMEM((tall, HEAD), bf16),
             pltpu.VMEM((2, half + 1, 2, rows, HEAD), bf16),
-            pltpu.VMEM((2, 2, 2, rows, HEAD), bf16),
+            pltpu.VMEM((2, half + 1, 2, rows, HEAD), bf16),
             pltpu.VMEM((tall, HEAD), bf16),
             pltpu.VMEM((QUAD, 1, HEAD), jnp.int32),
             dma((6,)), dma((2, ntp)), dma((2, ntp)), dma((2, half + 1)), dma((2, half + 1)),
@@ -388,7 +403,18 @@
     )(
         block_map, span_blocks.T, queries, keys, values, attn_out, out_grad, logsumexp, position_ids
     )
-    return together[:, :width], together[:, width : width + HEAD], together[:, width + HEAD :]
+    return pl.pallas_call(
+        divide_kernel,
+        out_shape=(
+            jax.ShapeDtypeStruct((rows, width), bf16),
+            jax.ShapeDtypeStruct((rows, HEAD), bf16),
+            jax.ShapeDtypeStruct((rows, HEAD), bf16),
+        ),
+        in_specs=[hbm],
+        out_specs=(hbm, hbm, hbm),
+        scratch_shapes=[dma((3,))],
+        name="divide_result",
+    )(together)
 
 
 def solution(mesh):

time: 80.3 us -> 93.2 us (1.16)
  Pallas kernels: 75.5 us -> 91.2 us
  local copies, waits for them, and re-layouts: 3.07 us -> 0 us
    pallas_call x0 -> x1, Pallas kernels: none -> 11.1 us  [shards(): pl.pallas_call(divide_kernel, out_shape=(jax.ShapeDtypeStruct((rows, widt...]
    pallas_call x1, Pallas kernels: 75.5 us -> 80.1 us  [shards(): pl.pallas_call(functools.partial(step_kernel, nz, ntp), out_shape=jax.Sha...]
    slice x2 -> x0, local copies, waits for them, and re-layouts: 3.07 us -> none  [the longest x1 1.67 us: shards(): together[:, :width]]
where the time goes in v6:
time: 93.2 us; the launch traced here: 91.8 us
  Pallas kernels  91.2 us (98%)
    pallas_call x1, Pallas kernels, shards(): pl.pallas_call(functools.partial(step_kernel, nz, ntp), out_shape=jax.Sha...  80.1 us
    pallas_call x1, Pallas kernels, shards(): pl.pallas_call(divide_kernel, out_shape=(jax.ShapeDtypeStruct((rows, widt...  11.1 us

profile of v6, /device:TPU:1, one launch (start us, length us, event | category | flops | bytes accessed | tf_op | source)
XLA Modules:
  0.0 91.8 jit_solution(10821432381769162058)
XLA Ops:
  0.6 80.1 %attention_backward.1.together = bf16[128,1280]{1,0:T(8,128)(2,1)} custom-call(s32[128]{0:T(128)} %map_in.1, s32[2,16]{1,0:T(2,128)} %bitcast.1, bf16[128,1024]{1,0:T(8,128)(2,1)} %q_in.1, bf16[128,128]{1,0:T(8,128)(2,1)} %k_in.1, bf16[128,128]{1,0:T(8,128)(2,1)} %v_in.1, bf16[128,1024]{1,0:T(8,128)(2,1)} %out_in.1, bf16[16,8192]{1,0:T(8,128)(2,1)} %grad_in.1, ...), custom_call_target="tpu_custom_call" | custom-call | tf_op jit(solution)/shard_map/attention_backward/pallas_call | solution.py:372
  80.8 11.1 %divide_result.1 = (bf16[128,1024]{1,0:T(8,128)(2,1)}, bf16[128,128]{1,0:T(8,128)(2,1)}, bf16[128,128]{1,0:T(8,128)(2,1)}) custom-call(bf16[128,1280]{1,0:T(8,128)(2,1)} %attention_backward.1.together), custom_call_target="tpu_custom_call" | custom-call | tf_op jit(solution)/shard_map/divide_result/pallas_call | solution.py:406

commit v7 on v5

--- a/solution.py
+++ b/solution.py
@@ -69,7 +69,8 @@
     core_peer = {"ctx": at_core, "tp": tp}
     y_peer = {"ctx": at_y, "tp": tp}
     cross_peer = {"ctx": at_core + 2 - 4 * yh, "tp": tp}
-    along = {k: {"ctx": (me + QUAD * k + n) % n, "tp": tp} for k in (1, 2, -1, -2)}
+    near = 3 if half >= 8 else 2
+    along = {k: {"ctx": (me + QUAD * k + n) % n, "tp": tp} for i in range(1, near + 2) for k in (i, -i)}
 
     loads = [
         pltpu.make_async_copy(source, target, local.at[i])
@@ -158,7 +159,6 @@
     q_core.start()
 
     arrived(1)
-    near = 3 if half >= 8 else (2 if half >= 4 else 1)
     for a in range(2, near + 1):
         arrived(a)
     later = list(range(near + 1, half - 1))
@@ -236,16 +236,16 @@
         )
 
     def start_chain(d, s, p, places):
-        at = far[d] - s
-        stage[d, at] = part_of(d, s, p).astype(jnp.bfloat16)
-        give(d, s, stage.at[d, at], places).start()
+        stage[d, s] = part_of(d, s, p).astype(jnp.bfloat16)
+        give(d, s, stage.at[d, s], places).start()
 
     def add_and_give(d, s, p, places):
-        give(d, s + 2, carry.at[d, s + 2], 1).wait_recv()
-        carry[d, s + 2] = (carry[d, s + 2].astype(jnp.float32) + part_of(d, s, p)).astype(jnp.bfloat16)
-        give(d, s, carry.at[d, s + 2], places).start()
+        give(d, s + 1, carry.at[d, s + 1], 1).wait_recv()
+        carry[d, s + 1] = (carry[d, s + 1].astype(jnp.float32) + part_of(d, s, p)).astype(jnp.bfloat16)
+        give(d, s, carry.at[d, s + 1], places).start()
 
     to_core = [send(dq_go.at[i], first.at[i], dq_send.at[i], dq_recv.at[i], core_peer) for i in range(2)]
+    to_y = send(back, second, dq_send.at[2], dq_recv.at[2], y_peer)
     span_rows = heads * HEAD
 
     def one_unit(u, unused):
@@ -291,38 +291,34 @@
             dq_go[0] = (dq[0, span_rows : 2 * span_rows, :] * scale).astype(jnp.bfloat16)
             to_core[0].start()
 
-        for d in range(2):
-            first_of = 2 * near + 2 * d + 1
-
-            @pl.when((u == first_of) | (u == first_of + 2))
+        for order_of in range(half - near):
+            place = half - order_of
+
+            @pl.when(u == 2 * (near + order_of) + 1)
             def _():
-                start_chain(d, s, p, 2)
-
-            if 2 * half > first_of + 4:
-
-                @pl.when((u >= first_of + 4) & (u % 2 == 1))
-                def _():
-                    add_and_give(d, s, p, 2)
+                for d in range(2):
+                    places = 1 if place - 1 > near else place
+                    if place + 1 <= far[d]:
+                        add_and_give(d, place, place % half, places)
+                    elif place <= far[d]:
+                        start_chain(d, place, place % half, places)
+                if order_of == 0:
+                    for a in range(1, near + 1):
+                        for d in range(2):
+                            start_chain(d, a, a, a)
 
         return unused
 
     lax.fori_loop(0, 2 * half, one_unit, 0)
+    to_core[0].wait_recv()
+    back[...] = (dq[0, 0:span_rows, :] * scale + first[0].astype(jnp.float32)).astype(jnp.bfloat16)
+    to_y.start()
     dq_go[1] = (dq[1, span_rows : 2 * span_rows, :] * scale).astype(jnp.bfloat16)
     to_core[1].start()
-    to_core[0].wait_recv()
-    back[...] = (dq[0, 0:span_rows, :] * scale + first[0].astype(jnp.float32)).astype(jnp.bfloat16)
-    to_y = send(back, second, dq_send.at[2], dq_recv.at[2], y_peer)
-    to_y.start()
-    for s in range(near, 0, -1):
-        for d in range(2):
-            if s + 2 <= far[d]:
-                add_and_give(d, s, s, min(s, 2))
-            elif s <= far[d]:
-                start_chain(d, s, s, min(s, 2))
     to_core[1].wait_recv()
     ends = [part[0, what, rows : 2 * rows, :] for what in range(2)]
     for d in range(2):
-        for s in (2, 1):
+        for s in range(1, near + 2):
             if s <= far[d]:
                 give(d, s, carry.at[d, s], 1).wait_recv()
                 ends = [ends[what] + carry[d, s, what].astype(jnp.float32) for what in range(2)]
@@ -374,7 +370,7 @@
             pltpu.VMEM((2, tall, HEAD), bf16),
             pltpu.VMEM((tall, HEAD), bf16),
             pltpu.VMEM((2, half + 1, 2, rows, HEAD), bf16),
-            pltpu.VMEM((2, 2, 2, rows, HEAD), bf16),
+            pltpu.VMEM((2, half + 1, 2, rows, HEAD), bf16),
             pltpu.VMEM((tall, HEAD), bf16),
             pltpu.VMEM((QUAD, 1, HEAD), jnp.int32),
             dma((6,)), dma((2, ntp)), dma((2, ntp)), dma((2, half + 1)), dma((2, half + 1)),

time: 80.3 us -> 83 us (1.034)
  the two profiles are of different devices: /device:TPU:1 before, /device:TPU:2 now
where the time goes in v7:
time: 83 us; the launch traced here: 82.7 us
  Pallas kernels  79 us (95%)
  local copies, waits for them, and re-layouts  3.07 us (4%)
    pallas_call x1, Pallas kernels, shards(): pl.pallas_call(functools.partial(step_kernel, nz, ntp), out_shape=jax.Sha...  79 us
    slice x1, local copies, waits for them, and re-layouts, shards(): together[:, :width]  1.67 us

profile of v7, /device:TPU:2, one launch (start us, length us, event | category | flops | bytes accessed | tf_op | source)
XLA Modules:
  0.0 82.7 jit_solution(5290004930512460062)
XLA Ops:
  0.6 79.0 %attention_backward.1 = bf16[128,1280]{1,0:T(8,128)(2,1)} custom-call(s32[128]{0:T(128)} %map_in.1, s32[2,16]{1,0:T(2,128)} %bitcast.1, bf16[128,1024]{1,0:T(8,128)(2,1)} %q_in.1, bf16[128,128]{1,0:T(8,128)(2,1)} %k_in.1, bf16[128,128]{1,0:T(8,128)(2,1)} %v_in.1, bf16[128,1024]{1,0:T(8,128)(2,1)} %out_in.1, bf16[16,8192]{1,0:T(8,128)(2,1)} %grad_in.1, ...), custom_call_target="tpu_custom_call" | custom-call | tf_op jit(solution)/shard_map/attention_backward/pallas_call | solution.py:353
  79.7 1.4 %fusion = (bf16[128,128]{1,0:T(8,128)(2,1)}, bf16[128,128]{1,0:T(8,128)(2,1)}) fusion(bf16[128,1280]{1,0:T(8,128)(2,1)} %attention_backward.1), kind=kLoop, calls=%fused_computation | loop fusion | bytes 131072 | tf_op jit(solution)/shard_map/slice | solution.py:387
  81.1 1.7 %slice.9 = bf16[128,1024]{1,0:T(8,128)(2,1)} slice(bf16[128,1280]{1,0:T(8,128)(2,1)} %attention_backward.1), slice={[0:128], [0:1024]} | slice | bytes 524288 | tf_op jit(solution)/shard_map/slice | solution.py:387
